TPU v7x, 1024 devices: a whole 4x8x16 slice. The times are simulated.
1024 devices in a mesh: row: 64 (over x, z), col: 16 (over y, core).
Axes of the slice: x: 4, y: 8, z: 16, core: 2. Of those that a mesh axis runs over, the one named last changes fastest.
Arguments:
- out_grad: bfloat16 [4096, 4096], P('col', 'row'), may hold values from -0.09375 to 0.09375
- inputs: bfloat16 [4096, 4096], P('row', 'col'), may hold values from -6 to 6
- left_root: bfloat16 [4096, 4096], P('row'), may hold values from -2 to 3, as said below
- right_root: bfloat16 [4096, 4096], P(None, 'col'), may hold values from -2 to 3, as said below
- momentum: float32 [4096, 4096], P('row', 'col'), may hold values from -6 to 6
Outputs:
- momentum_new: float32 [4096, 4096], P('row', 'col')
- update: bfloat16 [4096, 4096], P('row', 'col')
Inputs may be any that keep to these rules, and one draw needn't show every extreme that they name: `left_root`: symmetric. `right_root`: symmetric.
All inputs are finite; a program needn't handle non-finite values.
Results may differ from a plain program's by a relative error of at most 0.0057.
Values may be sent and summed in bfloat16 or wider, within the bound.
No kernel may reach another device: no remote copies, remote signals or barrier semaphores. Data moves between devices by JAX's collectives and lax.ppermute only.
A program may use at most 32 MiB of HBM per device.

v0:
```python
import jax
import jax.numpy as jnp
from jax import lax
from jax.sharding import Mesh
from jax.sharding import PartitionSpec as P

ROW = ("row_0", "row_1")


def copy_for_each(shard, axis):
    copies = jnp.broadcast_to(shard, (lax.axis_size(axis), *shard.shape))
    return lax.all_to_all(copies, axis, split_axis=0, concat_axis=0, tiled=True)


def in_order(parts, dim):
    parts = jnp.moveaxis(parts, 0, dim)
    shape = parts.shape
    return parts.reshape(*shape[:dim], shape[dim] * shape[dim + 1], *shape[dim + 2 :])


def gathered_copies(shard, axis, dim):
    parts = copy_for_each(shard, axis)
    return in_order(parts, dim)


def stacked_from(shard, axes, order):
    parts = shard[None]
    for k in order:
        parts = lax.all_gather(parts, axes[k], axis=0, tiled=True)
    carried = [lax.axis_size(axes[k]) for k in reversed(order)]
    parts = parts.reshape(*carried, *shard.shape)
    turned = sorted(range(len(order)), key=lambda place: order[len(order) - 1 - place])
    return parts.transpose(*turned, *range(len(order), parts.ndim)).reshape(-1, *shard.shape)


def whole_of(shard, axes, order, dim):
    return in_order(stacked_from(shard, axes, order), dim)


def body(out_grad, inputs, left_root, right_root, momentum):
    cotangent = gathered_copies(out_grad, "col", 0)
    grad_tile = lax.dot_general(
        cotangent,
        whole_of(inputs, ROW, (0, 1), 0),
        (((0,), (0,)), ((), ())),
        preferred_element_type=jnp.float32,
    ).astype(jnp.bfloat16)
    first = jnp.dot(
        left_root,
        lax.all_gather(grad_tile, ROW, axis=0, tiled=True),
        preferred_element_type=jnp.float32,
    )
    first = first.astype(jnp.bfloat16)
    shaped = jnp.dot(
        gathered_copies(first, "col", 1), right_root, preferred_element_type=jnp.float32
    )
    momentum_new = 0.9 * momentum + shaped
    update = (0.25 * (0.9 * momentum_new + shaped)).astype(jnp.bfloat16)
    return (momentum_new, update)


def solution(mesh):
    split = Mesh(mesh.devices.reshape(4, 16, mesh.shape["col"]), ("row_0", "row_1", "col"))
    in_specs = (P("col", ROW), P(ROW, "col"), P(ROW, None), P(None, "col"), P(ROW, "col"))
    out_specs = (P(ROW, "col"), P(ROW, "col"))
    return jax.shard_map(body, mesh=split, in_specs=in_specs, out_specs=out_specs, check_vma=False)
```

profile of v0, /device:TPU:1, one launch (start us, length us, event | category | flops | bytes accessed | tf_op | source)
XLA Modules:
  0.0 289.3 jit_solution(8015822943566169668)
XLA Ops:
  7.2 0.0 copy-start
  7.2 0.0 all-gather.4.cloned.1.call-start
  7.2 12.2 %all-gather = bf16[256,256]{1,0:T(8,128)(2,1)} all-gather(bf16[64,256]{1,0:T(8,128)(2,1)} %param.6), channel_id=2, replica_groups=mesh['row_0'=4,'row_1'=16,'col'=16] {'row_0'}, dimensions={0}, use_global_device_ids=true | all-gather | bytes 163840 | tf_op jit(solution)/shard_map/all_gather | solution.py:29
  19.4 0.0 all-gather.4.cloned.1.call-update
  19.4 0.0 all-gather.6.cloned.1.call-start
  19.5 0.8 broadcast_in_dim.9
  20.3 34.8 %all_to_all.10 = bf16[16,256,64]{1,2,0:T(8,128)(2,1)S(1)} all-to-all(bf16[16,256,64]{1,2,0:T(8,128)(2,1)S(1)} %broadcast_in_dim.9), channel_id=1, replica_groups=mesh['row_0'=4,'row_1'=16,'col'=16] {'col'}, dimensions={0} | all-to-all | bytes 1048576 | tf_op jit(solution)/shard_map/all_to_all | solution.py:12
  55.1 40.9 %all-gather.4.cloned.1.call-done = bf16[64,64,256]{2,1,0:T(8,128)(2,1)} async-done(((bf16[4,64,256]{2,1,0:T(8,128)(2,1)}), bf16[64,64,256]{2,1,0:T(8,128)(2,1)}) %all-gather.4.cloned.1.call-update) | async-done | bytes 2097168 | tf_op jit(solution)/shard_map/all_gather | solution.py:29
  96.0 1.7 copy.14
  97.7 0.0 copy-start.1
  97.7 1.1 convolution_convert_fusion.1
  98.8 0.0 all-gather.6.cloned.1.call-update
  98.8 0.0 copy-start.2
  98.8 146.7 %all-gather.6.cloned.1.call-done = bf16[4096,256]{1,0:T(8,128)(2,1)} async-done(((bf16[64,256]{1,0:T(8,128)(2,1)}), bf16[4096,256]{1,0:T(8,128)(2,1)}) %all-gather.6.cloned.1.call-update) | async-done | bytes 2097168 | tf_op jit(solution)/shard_map/all_gather | solution.py:50
  245.5 0.0 copy-done.1
  245.5 2.1 fusion
  247.6 0.1 broadcast_in_dim.11
  247.6 33.6 %all_to_all.11 = bf16[16,64,256]{2,1,0:T(8,128)(2,1)S(1)} all-to-all(bf16[16,64,256]{2,1,0:T(8,128)(2,1)S(1)} %broadcast_in_dim.11), channel_id=1, replica_groups=mesh['row_0'=4,'row_1'=16,'col'=16] {'col'}, dimensions={0} | all-to-all | bytes 1048576 | tf_op jit(solution)/shard_map/all_to_all | solution.py:12
  281.3 0.0 copy-done
  281.3 0.0 copy-done.2
  281.3 1.1 multiply_convert_fusion
  (2 shorter events, 0.1 us)
Async XLA Ops:
  7.2 274.1 %copy-start = (bf16[4096,256]{1,0:T(8,128)(2,1)S(1)}, bf16[4096,256]{1,0:T(8,128)(2,1)}, u32[]{:S(2)}) copy-start(bf16[4096,256]{1,0:T(8,128)(2,1)} %param.8) | copy-start | bytes 6291460
  7.2 88.8 %all-gather.4.cloned.1.call-start = ((), (), s32[]{:S(2)}) async-start(), calls=%async_computation.2 | async-start | bytes 2228224 | tf_op jit(solution)/shard_map/all_gather | solution.py:29
  19.4 226.1 %all-gather.6.cloned.1.call-start = ((), (), s32[]{:S(2)}) async-start(), calls=%async_computation.3 | async-start | bytes 2129920 | tf_op jit(solution)/shard_map/all_gather | solution.py:50
  97.7 147.8 %copy-start.1 = (bf16[64,4096]{1,0:T(8,128)(2,1)S(1)}, bf16[64,4096]{1,0:T(8,128)(2,1)}, u32[]{:S(2)}) copy-start(bf16[64,4096]{1,0:T(8,128)(2,1)} %param.7) | copy-start | bytes 1572868
  98.8 182.5 %copy-start.2 = (f32[64,256]{1,0:T(8,128)S(1)}, f32[64,256]{1,0:T(8,128)}, u32[]{:S(2)}) copy-start(f32[64,256]{1,0:T(8,128)} %param.9) | copy-start | bytes 196612
Sparse Core Ops, SparseCore 0:
  19.5 76.3 all-gather.3
  100.6 144.8 all-gather.5
where the time goes:
time: 290 us; the launch traced here: 289 us
  waiting for transfers between devices  188 us (65%)
  blocking collectives  80.6 us (28%)
  between operations  14.1 us (5%)
  matrix products  4.26 us (1%)
    all_gather x1, waiting for transfers between devices, body(): lax.all_gather(grad_tile, ROW, axis=0, tiled=True)  147 us
    all_to_all x2, blocking collectives, copy_for_each(): return lax.all_to_all(copies, axis, split_axis=0, concat_axis=0, tiled=True)  68.4 us
    all_gather x1, waiting for transfers between devices, stacked_from(): parts = lax.all_gather(parts, axes[k], axis=0, tiled=True)  40.9 us
    all_gather x1, blocking collectives, stacked_from(): parts = lax.all_gather(parts, axes[k], axis=0, tiled=True)  12.2 us
  transfers between devices with their start and end apart: 2, of which 2 were waited for; matrix products, arithmetic and copies ran while one was open for 0% of the time, Pallas kernels for 0%

commit v1 on v0

v1 whole, which is shorter than its diff:
```python
import jax
import jax.numpy as jnp
from jax import lax
from jax.sharding import Mesh
from jax.sharding import PartitionSpec as P

ROW = ("x", "z")
COL = "col"


def contract(a, b, da, db):
    return lax.dot_general(a, b, (((da,), (db,)), ((), ())), preferred_element_type=jnp.float32)


def summed_over_x(parts):
    parts = lax.all_to_all(parts.astype(jnp.bfloat16), "x", 0, 0)
    total = parts[0].astype(jnp.float32)
    for k in range(1, parts.shape[0]):
        total += parts[k].astype(jnp.float32)
    return total.astype(jnp.bfloat16)


def body(out_grad, inputs, left_root, right_root, momentum):
    nx, nz = lax.axis_size("x"), lax.axis_size("z")
    rows, order = left_root.shape
    cols = inputs.shape[1]
    wide = order // nx
    lows = nz // nx

    turn = []
    for x in range(nx):
        for high in range(lows):
            for low in range(nx):
                turn.append((x * nz + high * nx + low, low * nz + high * nx + x))
    turned = lax.ppermute(inputs, ROW, turn)

    left = lax.all_to_all(left_root.reshape(rows, nx, wide).transpose(1, 0, 2), "x", 0, 0)
    left = left.reshape(nx * rows, wide)

    tokens = lax.all_to_all(jnp.broadcast_to(turned, (nz, rows, cols)), "z", 0, 0)
    tokens = tokens.reshape(lows, nx, rows, cols).transpose(1, 0, 2, 3).reshape(-1, cols)

    cotangent = lax.all_gather(out_grad.T, "z", axis=0, tiled=True)
    part = contract(cotangent, left, 0, 1)
    product = summed_over_x(part.reshape(nx, rows, nx * rows))
    panel = lax.all_gather(product, COL, axis=0, tiled=True)

    part = contract(panel, tokens, 0, 0)
    first = summed_over_x(part.reshape(nx, rows, cols))
    panel = lax.all_gather(first, COL, axis=0)
    panel = panel.transpose(1, 0, 2).reshape(rows, -1)
    shaped = contract(panel, right_root, 1, 0)
    momentum_new = 0.9 * momentum + shaped
    update = (0.25 * (0.9 * momentum_new + shaped)).astype(jnp.bfloat16)
    return (momentum_new, update)


def solution(mesh):
    split = Mesh(mesh.devices.reshape(4, 16, mesh.shape["col"]), ("x", "z", "col"))
    in_specs = (P("col", ROW), P(ROW, "col"), P(ROW, None), P(None, "col"), P(ROW, "col"))
    out_specs = (P(ROW, "col"), P(ROW, "col"))
    return jax.shard_map(body, mesh=split, in_specs=in_specs, out_specs=out_specs, check_vma=False)
```

time: 290 us -> 133 us (0.46)
  waiting for transfers between devices: 188 us -> 4.16 us
  blocking collectives: 80.6 us -> 104 us
  starting transfers between devices: 0.08 us -> 16.3 us
  between operations: 14.1 us -> 0.76 us
    all_gather x2 -> x0, waiting for transfers between devices: 188 us -> none  [the longest x1 147 us: body(): lax.all_gather(grad_tile, ROW, axis=0, tiled=True)]
    all_gather x1 -> x3, blocking collectives: 12.2 us -> 90.6 us  [the longest x1 40.7 us: body(): cotangent = lax.all_gather(out_grad.T, 'z', axis=0, tiled=True)]
    all_to_all x2 -> x1, blocking collectives: 68.4 us -> 13 us  [summed_over_x(): parts = lax.all_to_all(parts.astype(jnp.bfloat16), 'x', 0, 0)]
    all_to_all x0 -> x3, starting transfers between devices: none -> 15.6 us  [the longest x1 6.2 us: body(): lax.all_to_all(jnp.broadcast_to(turned, (nz, rows, cols)), 'z', 0, 0)]
    all_to_all x0 -> x3, waiting for transfers between devices: none -> 4.16 us  [the longest x1 4.15 us: summed_over_x(): parts = lax.all_to_all(parts.astype(jnp.bfloat16), 'x', 0, 0)]
  transfers between devices with their start and end apart: 2 -> 4, of which waited for: 2 -> 1; matrix products, arithmetic and copies ran while one was open for 0% -> 2% of each run, Pallas kernels for 0% -> 0%
where the time goes in v1:
time: 133 us
  blocking collectives  104 us (78%)
  starting transfers between devices  16.3 us (12%)
  local copies, waits for them, and re-layouts  5.45 us (4%)
  waiting for transfers between devices  4.16 us (3%)
  matrix products  2.39 us (2%)
    all_gather x1, blocking collectives, body(): cotangent = lax.all_gather(out_grad.T, 'z', axis=0, tiled=True)  40.7 us
    all_gather x1, blocking collectives, body(): panel = lax.all_gather(product, COL, axis=0, tiled=True)  32.1 us
    all_gather x1, blocking collectives, body(): panel = lax.all_gather(first, COL, axis=0)  17.8 us
    all_to_all x1, blocking collectives, summed_over_x(): parts = lax.all_to_all(parts.astype(jnp.bfloat16), 'x', 0, 0)  13 us
    all_to_all x1, starting transfers between devices, body(): lax.all_to_all(jnp.broadcast_to(turned, (nz, rows, cols)), 'z', 0, 0)  6.2 us
    all_to_all x1, starting transfers between devices, body(): lax.all_to_all(left_root.reshape(rows, nx, wide).transpose(1, 0, 2), 'x',...  4.96 us
    all_to_all x1, starting transfers between devices, summed_over_x(): parts = lax.all_to_all(parts.astype(jnp.bfloat16), 'x', 0, 0)  4.45 us
    all_to_all x1, waiting for transfers between devices, summed_over_x(): parts = lax.all_to_all(parts.astype(jnp.bfloat16), 'x', 0, 0)  4.15 us
  transfers between devices with their start and end apart: 4, of which 1 were waited for; matrix products, arithmetic and copies ran while one was open for 2% of the time, Pallas kernels for 0%

profile of v1, /device:TPU:1, one launch (start us, length us, event | category | flops | bytes accessed | tf_op | source)
XLA Modules:
  0.0 132.7 jit_solution(3212320035489829878)
XLA Ops:
  0.6 0.0 copy-start
  0.6 0.0 copy-start.2
  0.7 2.0 %copy.23 = bf16[8,4,8,1024]{3,2,0,1:T(8,128)(2,1)} copy(bf16[8,4,8,1024]{3,2,1,0:T(8,128)(2,1)} %bitcast.41) | data formatting | bytes 1048576 | tf_op jit(solution)/shard_map/reshape | solution.py:37
  2.7 0.0 copy-start.3
  2.7 5.0 %all-to-all-start = ((bf16[4,64,1024]{2,1,0:T(8,128)(2,1)}), bf16[4,64,1024]{2,1,0:T(8,128)(2,1)S(1)}, u32[]{:S(2)}, u32[]{:S(2)}) async-start(bf16[4,64,1024]{2,1,0:T(8,128)(2,1)} %bitcast.31), calls=%async_computation | async-start | bytes 1048576 | tf_op jit(solution)/shard_map/all_to_all | solution.py:37
  7.6 0.0 copy-done.2
  7.6 40.7 %all_gather.10 = bf16[1024,256]{1,0:T(8,128)(2,1)} all-gather(bf16[64,256]{1,0:T(8,128)(2,1)S(1)} %bitcast.42), channel_id=1, replica_groups=mesh['x'=4,'z'=16,'col'=16] {'z'}, dimensions={0}, use_global_device_ids=true | all-gather | bytes 557056 | tf_op jit(solution)/shard_map/all_gather | solution.py:43
  48.4 1.2 copy.15
  49.6 0.0 all-to-all-done
  49.6 1.0 convolution_convert_fusion.1
  50.6 4.5 %all-to-all-start.1 = ((bf16[4,64,256]{2,1,0:T(8,128)(2,1)}), bf16[4,64,256]{2,1,0:T(8,128)(2,1)S(1)}, u32[]{:S(2)}, u32[]{:S(2)}) async-start(bf16[4,64,256]{2,1,0:T(8,128)(2,1)} %convolution_convert_fusion.1), calls=%async_computation.1 | async-start | bytes 262144 | tf_op jit(solution)/shard_map/all_to_all | solution.py:16
  55.1 0.0 copy-done.3
  55.1 0.7 collective-permute-start
  55.7 0.0 collective-permute-done
  55.7 4.2 %all-to-all-done.1 = bf16[4,64,256]{2,1,0:T(8,128)(2,1)S(1)} async-done(((bf16[4,64,256]{2,1,0:T(8,128)(2,1)}), bf16[4,64,256]{2,1,0:T(8,128)(2,1)S(1)}, u32[]{:S(2)}, u32[]{:S(2)}) %all-to-all-start.1) | async-done | bytes 131104 | tf_op jit(solution)/shard_map/all_to_all | solution.py:16
  59.9 0.8 broadcast_in_dim.3
  60.7 6.2 %all-to-all-start.2 = ((bf16[16,64,256]{2,1,0:T(8,128)(2,1)}), bf16[16,64,256]{2,1,0:T(8,128)(2,1)S(1)}, u32[]{:S(2)}, u32[]{:S(2)}) async-start(bf16[16,64,256]{2,1,0:T(8,128)(2,1)} %broadcast_in_dim.3), calls=%async_computation.2 | async-start | bytes 1048576 | tf_op jit(solution)/shard_map/all_to_all | solution.py:40
  67.0 32.1 %all-gather = bf16[1,1024,256]{2,1,0:T(8,128)(2,1)} all-gather(bf16[1,64,256]{2,1,0:T(8,128)(2,1)S(1)} %add_convert_fusion.1), channel_id=2, replica_groups=mesh['x'=4,'z'=16,'col'=16] {'col'}, dimensions={1}, use_global_device_ids=true | all-gather | bytes 557056 | tf_op jit(solution)/shard_map/all_gather | solution.py:46
  99.1 1.2 copy.17
  100.3 0.0 all-to-all-done.2
  100.3 0.0 copy-start.1
  100.4 0.3 convolution_convert_fusion
  100.7 13.0 %all_to_all.20 = bf16[4,64,256]{2,1,0:T(8,128)(2,1)S(1)} all-to-all(bf16[4,64,256]{2,1,0:T(8,128)(2,1)S(1)} %convolution_convert_fusion), channel_id=1, replica_groups=mesh['x'=4,'z'=16,'col'=16] {'x'}, dimensions={0} | all-to-all | bytes 262144 | tf_op jit(solution)/shard_map/all_to_all | solution.py:16
  113.7 17.8 %all_gather.12 = bf16[16,64,256]{2,1,0:T(8,128)(2,1)S(1)} all-gather(bf16[1,64,256]{2,1,0:T(8,128)(2,1)S(1)} %add_convert_fusion), channel_id=1, replica_groups=mesh['x'=4,'z'=16,'col'=16] {'col'}, dimensions={0}, use_global_device_ids=true | all-gather | bytes 557056 | tf_op jit(solution)/shard_map/all_gather | solution.py:50
  131.6 0.0 copy-done
  131.6 0.0 copy-done.1
  131.6 1.1 multiply_convert_fusion
  (4 shorter events, 0.1 us)
Async XLA Ops:
  0.6 130.9 %copy-start = (bf16[4096,256]{1,0:T(8,128)(2,1)S(1)}, bf16[4096,256]{1,0:T(8,128)(2,1)}, u32[]{:S(2)}) copy-start(bf16[4096,256]{1,0:T(8,128)(2,1)} %param.8) | copy-start | bytes 6291460
  0.6 7.0 %copy-start.2 = (bf16[256,64]{0,1:T(8,128)(2,1)S(1)}, bf16[256,64]{0,1:T(8,128)(2,1)}, u32[]{:S(2)}) copy-start(bf16[256,64]{0,1:T(8,128)(2,1)} %param.5) | copy-start | bytes 98308
  2.7 52.4 %copy-start.3 = (bf16[64,256]{1,0:T(8,128)(2,1)S(1)}, bf16[64,256]{1,0:T(8,128)(2,1)}, u32[]{:S(2)}) copy-start(bf16[64,256]{1,0:T(8,128)(2,1)} %param.6) | copy-start | bytes 98308
  2.7 46.9 %all-to-all-start = ((bf16[4,64,1024]{2,1,0:T(8,128)(2,1)}), bf16[4,64,1024]{2,1,0:T(8,128)(2,1)S(1)}, u32[]{:S(2)}, u32[]{:S(2)}) async-start(bf16[4,64,1024]{2,1,0:T(8,128)(2,1)} %bitcast.31), calls=%async_computation | async-start | bytes 1048576 | tf_op jit(solution)/shard_map/all_to_all | solution.py:37
  50.6 9.3 %all-to-all-start.1 = ((bf16[4,64,256]{2,1,0:T(8,128)(2,1)}), bf16[4,64,256]{2,1,0:T(8,128)(2,1)S(1)}, u32[]{:S(2)}, u32[]{:S(2)}) async-start(bf16[4,64,256]{2,1,0:T(8,128)(2,1)} %convolution_convert_fusion.1), calls=%async_computation.1 | async-start | bytes 262144 | tf_op jit(solution)/shard_map/all_to_all | solution.py:16
  55.1 0.7 collective-permute-start
  60.7 39.6 %all-to-all-start.2 = ((bf16[16,64,256]{2,1,0:T(8,128)(2,1)}), bf16[16,64,256]{2,1,0:T(8,128)(2,1)S(1)}, u32[]{:S(2)}, u32[]{:S(2)}) async-start(bf16[16,64,256]{2,1,0:T(8,128)(2,1)} %broadcast_in_dim.3), calls=%async_computation.2 | async-start | bytes 1048576 | tf_op jit(solution)/shard_map/all_to_all | solution.py:40
  100.3 31.2 %copy-start.1 = (f32[64,256]{1,0:T(8,128)S(1)}, f32[64,256]{1,0:T(8,128)}, u32[]{:S(2)}) copy-start(f32[64,256]{1,0:T(8,128)} %param.9) | copy-start | bytes 196612

commit v2 on v1

v2 whole, which is shorter than its diff:
```python
import jax
import jax.numpy as jnp
from jax import lax
from jax.sharding import Mesh
from jax.sharding import PartitionSpec as P

ROW = ("x", "z")
COL = "col"


def contract(a, b, da, db):
    return lax.dot_general(a, b, (((da,), (db,)), ((), ())), preferred_element_type=jnp.float32)


def summed_over_x(parts):
    parts = lax.all_to_all(parts, "x", 0, 0)
    total = parts[0].astype(jnp.float32)
    for k in range(1, parts.shape[0]):
        total += parts[k].astype(jnp.float32)
    return total.astype(jnp.bfloat16)


def body(out_grad, inputs, left_root, right_root, momentum):
    nx, nz = lax.axis_size("x"), lax.axis_size("z")
    rows, order = left_root.shape
    cols = inputs.shape[1]
    wide = order // nx

    share = rows // nx
    half = share // 2
    rest = jnp.zeros((half, wide - 2 * cols), inputs.dtype)
    blocks = []
    for x in range(nx):
        own = inputs[x * share : (x + 1) * share]
        own = jnp.concatenate([own[:half], own[half:], rest], axis=1)
        blocks.append(jnp.concatenate([left_root[:, x * wide : (x + 1) * wide], own], axis=0))
    with jax.named_scope("turn"):
        got = lax.all_to_all(jnp.stack(blocks), "x", 0, 0)
    left = got[:, :rows].reshape(nx * rows, wide)
    own = got[:, rows:]
    own = jnp.stack([own[:, :, :cols], own[:, :, cols : 2 * cols]], axis=1)

    cotangent = lax.all_gather(out_grad.T, "z", axis=0, tiled=True)

    own = jnp.broadcast_to(own.reshape(rows, cols), (nz, rows, cols))
    with jax.named_scope("tokens"):
        tokens = lax.all_to_all(own, "z", 0, 0)
    tokens = tokens.reshape(nz, nx, share, cols).transpose(1, 0, 2, 3).reshape(-1, cols)

    part = contract(cotangent, left, 0, 1).astype(jnp.bfloat16)
    part = part.reshape(-1, nx, share, nx * rows).transpose(1, 0, 2, 3).reshape(nx, -1, nx * rows)
    with jax.named_scope("product"):
        product = summed_over_x(part)
    panel = lax.all_gather(product, COL, axis=0, tiled=True)

    part = contract(panel, tokens, 0, 0).astype(jnp.bfloat16).reshape(nx, rows, cols)
    first = summed_over_x(part)
    panel = lax.all_gather(first, COL, axis=0)
    panel = panel.transpose(1, 0, 2).reshape(rows, -1)
    shaped = contract(panel, right_root, 1, 0)
    momentum_new = 0.9 * momentum + shaped
    update = (0.25 * (0.9 * momentum_new + shaped)).astype(jnp.bfloat16)
    return (momentum_new, update)


def solution(mesh):
    split = Mesh(mesh.devices.reshape(4, 16, mesh.shape["col"]), ("x", "z", "col"))
    in_specs = (P("col", ROW), P(ROW, "col"), P(ROW, None), P(None, "col"), P(ROW, "col"))
    out_specs = (P(ROW, "col"), P(ROW, "col"))
    return jax.shard_map(body, mesh=split, in_specs=in_specs, out_specs=out_specs, check_vma=False)
```

time: 133 us -> 121 us (0.910)
  blocking collectives: 104 us -> 96.1 us
  starting transfers between devices: 16.3 us -> 12.5 us
  local copies, waits for them, and re-layouts: 5.45 us -> 3.73 us
    all_to_all x1, blocking collectives: 13 us -> 7.21 us  [summed_over_x(): parts = lax.all_to_all(parts, 'x', 0, 0)]
    all_gather x1, blocking collectives: 17.8 us -> 21.5 us  [body(): panel = lax.all_gather(first, COL, axis=0)]
    all_gather x1, blocking collectives: 32.1 us -> 28.5 us  [body(): panel = lax.all_gather(product, COL, axis=0, tiled=True)]
    all_to_all x3, starting transfers between devices: 15.6 us -> 12.5 us  [the longest x1 4.83 us: body(): got = lax.all_to_all(jnp.stack(blocks), 'x', 0, 0)]
    dot_general x2 -> x0, local copies, waits for them, and re-layouts: 2.49 us -> none  [contract(): lax.dot_general(a, b, (((da,), (db,)), ((), ())), preferred_element_type=...]
    slice x0 -> x3, local copies, waits for them, and re-layouts: none -> 2.13 us  [the longest x1 1.14 us: body(): left_root[:, x * wide:(x + 1) * wide]]
    all_gather x1, blocking collectives: 40.7 us -> 38.9 us  [body(): cotangent = lax.all_gather(out_grad.T, 'z', axis=0, tiled=True)]
    reshape x1, local copies, waits for them, and re-layouts: 2.02 us -> 0.66 us  [body(): part.reshape(-1, nx, share, nx * rows).transpose(1, 0, 2, 3)]
  transfers between devices with their start and end apart: 4 -> 3, of which waited for: 1 -> 1; matrix products, arithmetic and copies ran while one was open for 2% -> 0% of each run, Pallas kernels for 0% -> 0%
where the time goes in v2:
time: 121 us
  blocking collectives  96.1 us (79%)
  starting transfers between devices  12.5 us (10%)
  waiting for transfers between devices  4.82 us (4%)
  local copies, waits for them, and re-layouts  3.73 us (3%)
  matrix products  1.8 us (1%)
    all_gather x1, blocking collectives, body(): cotangent = lax.all_gather(out_grad.T, 'z', axis=0, tiled=True)  38.9 us
    all_gather x1, blocking collectives, body(): panel = lax.all_gather(product, COL, axis=0, tiled=True)  28.5 us
    all_gather x1, blocking collectives, body(): panel = lax.all_gather(first, COL, axis=0)  21.5 us
    all_to_all x1, blocking collectives, summed_over_x(): parts = lax.all_to_all(parts, 'x', 0, 0)  7.21 us
    all_to_all x1, starting transfers between devices, body(): got = lax.all_to_all(jnp.stack(blocks), 'x', 0, 0)  4.83 us
    all_to_all x1, waiting for transfers between devices, summed_over_x(): parts = lax.all_to_all(parts, 'x', 0, 0)  4.81 us
    all_to_all x1, starting transfers between devices, body(): tokens = lax.all_to_all(own, 'z', 0, 0)  3.86 us
    all_to_all x1, starting transfers between devices, summed_over_x(): parts = lax.all_to_all(parts, 'x', 0, 0)  3.8 us
  transfers between devices with their start and end apart: 3, of which 1 were waited for; matrix products, arithmetic and copies ran while one was open for 0% of the time, Pallas kernels for 0%

profile of v2, /device:TPU:1, one launch (start us, length us, event | category | flops | bytes accessed | tf_op | source)
XLA Modules:
  0.0 120.7 jit_solution(16176697049658480167)
XLA Ops:
  0.6 0.0 copy-start
  0.6 1.0 fusion.10
  1.6 0.0 copy-start.2
  1.6 1.1 fusion.9
  2.8 0.9 pad_maximum_fusion
  3.7 4.8 %all-to-all-start = ((bf16[4,72,1024]{2,1,0:T(8,128)(2,1)}), bf16[4,72,1024]{2,1,0:T(8,128)(2,1)S(1)}, u32[]{:S(2)}, u32[]{:S(2)}) async-start(bf16[4,72,1024]{2,1,0:T(8,128)(2,1)} %pad_maximum_fusion), calls=%async_computation | async-start | bytes 1179648 | tf_op jit(solution)/shard_map/turn/all_to_all | solution.py:38
  8.5 0.0 copy-done.2
  8.5 38.9 %all_gather.10 = bf16[1024,256]{1,0:T(8,128)(2,1)S(1)} all-gather(bf16[64,256]{1,0:T(8,128)(2,1)S(1)} %bitcast.47), channel_id=1, replica_groups=mesh['x'=4,'z'=16,'col'=16] {'z'}, dimensions={0}, use_global_device_ids=true | all-gather | bytes 557056 | tf_op jit(solution)/shard_map/all_gather | solution.py:43
  47.5 0.0 all-to-all-done
  47.5 0.4 convolution_convert_fusion.1
  47.9 0.7 copy.14
  48.5 3.8 %all-to-all-start.1 = ((bf16[4,64,256]{2,1,0:T(8,128)(2,1)}), bf16[4,64,256]{2,1,0:T(8,128)(2,1)S(1)}, u32[]{:S(2)}, u32[]{:S(2)}) async-start(bf16[4,64,256]{2,1,0:T(8,128)(2,1)} %bitcast.9), calls=%async_computation.1 | async-start | bytes 262144 | tf_op jit(solution)/shard_map/product/all_to_all | solution.py:16
  52.3 4.8 %all-to-all-done.1 = bf16[4,64,256]{2,1,0:T(8,128)(2,1)S(1)} async-done(((bf16[4,64,256]{2,1,0:T(8,128)(2,1)}), bf16[4,64,256]{2,1,0:T(8,128)(2,1)S(1)}, u32[]{:S(2)}, u32[]{:S(2)}) %all-to-all-start.1) | async-done | bytes 131104 | tf_op jit(solution)/shard_map/product/all_to_all | solution.py:16
  57.2 0.8 broadcast_in_dim.7
  58.0 3.9 %all-to-all-start.2 = ((bf16[16,64,256]{2,1,0:T(8,128)(2,1)}), bf16[16,64,256]{2,1,0:T(8,128)(2,1)S(1)}, u32[]{:S(2)}, u32[]{:S(2)}) async-start(bf16[16,64,256]{2,1,0:T(8,128)(2,1)} %broadcast_in_dim.7), calls=%async_computation.2 | async-start | bytes 1048576 | tf_op jit(solution)/shard_map/tokens/all_to_all | solution.py:47
  61.9 28.5 %all-gather = bf16[1,1024,256]{2,1,0:T(8,128)(2,1)S(1)} all-gather(bf16[1,64,256]{2,1,0:T(8,128)(2,1)S(1)} %add_convert_fusion.1), channel_id=2, replica_groups=mesh['x'=4,'z'=16,'col'=16] {'col'}, dimensions={1}, use_global_device_ids=true | all-gather | bytes 557056 | tf_op jit(solution)/shard_map/all_gather | solution.py:54
  90.4 0.0 all-to-all-done.2
  90.4 0.0 copy-start.1
  90.4 0.3 convolution_convert_fusion
  90.8 7.2 %all_to_all.20 = bf16[4,64,256]{2,1,0:T(8,128)(2,1)S(1)} all-to-all(bf16[4,64,256]{2,1,0:T(8,128)(2,1)S(1)} %bitcast.46), channel_id=1, replica_groups=mesh['x'=4,'z'=16,'col'=16] {'x'}, dimensions={0} | all-to-all | bytes 262144 | tf_op jit(solution)/shard_map/all_to_all | solution.py:16
  98.0 21.5 %all_gather.12 = bf16[16,64,256]{2,1,0:T(8,128)(2,1)S(1)} all-gather(bf16[1,64,256]{2,1,0:T(8,128)(2,1)S(1)} %add_convert_fusion), channel_id=1, replica_groups=mesh['x'=4,'z'=16,'col'=16] {'col'}, dimensions={0}, use_global_device_ids=true | all-gather | bytes 557056 | tf_op jit(solution)/shard_map/all_gather | solution.py:58
  119.6 0.0 copy-done
  119.6 0.0 copy-done.1
  119.6 1.1 multiply_convert_fusion
  (9 shorter events, 0.2 us)
Async XLA Ops:
  0.6 118.9 %copy-start = (bf16[4096,256]{1,0:T(8,128)(2,1)S(1)}, bf16[4096,256]{1,0:T(8,128)(2,1)}, u32[]{:S(2)}) copy-start(bf16[4096,256]{1,0:T(8,128)(2,1)} %param.8) | copy-start | bytes 6291460
  1.6 6.9 %copy-start.2 = (bf16[256,64]{0,1:T(8,128)(2,1)S(1)}, bf16[256,64]{0,1:T(8,128)(2,1)}, u32[]{:S(2)}) copy-start(bf16[256,64]{0,1:T(8,128)(2,1)} %param.5) | copy-start | bytes 98308
  3.7 43.8 %all-to-all-start = ((bf16[4,72,1024]{2,1,0:T(8,128)(2,1)}), bf16[4,72,1024]{2,1,0:T(8,128)(2,1)S(1)}, u32[]{:S(2)}, u32[]{:S(2)}) async-start(bf16[4,72,1024]{2,1,0:T(8,128)(2,1)} %pad_maximum_fusion), calls=%async_computation | async-start | bytes 1179648 | tf_op jit(solution)/shard_map/turn/all_to_all | solution.py:38
  48.5 8.6 %all-to-all-start.1 = ((bf16[4,64,256]{2,1,0:T(8,128)(2,1)}), bf16[4,64,256]{2,1,0:T(8,128)(2,1)S(1)}, u32[]{:S(2)}, u32[]{:S(2)}) async-start(bf16[4,64,256]{2,1,0:T(8,128)(2,1)} %bitcast.9), calls=%async_computation.1 | async-start | bytes 262144 | tf_op jit(solution)/shard_map/product/all_to_all | solution.py:16
  58.0 32.4 %all-to-all-start.2 = ((bf16[16,64,256]{2,1,0:T(8,128)(2,1)}), bf16[16,64,256]{2,1,0:T(8,128)(2,1)S(1)}, u32[]{:S(2)}, u32[]{:S(2)}) async-start(bf16[16,64,256]{2,1,0:T(8,128)(2,1)} %broadcast_in_dim.7), calls=%async_computation.2 | async-start | bytes 1048576 | tf_op jit(solution)/shard_map/tokens/all_to_all | solution.py:47
  90.4 29.2 %copy-start.1 = (f32[64,256]{1,0:T(8,128)S(1)}, f32[64,256]{1,0:T(8,128)}, u32[]{:S(2)}) copy-start(f32[64,256]{1,0:T(8,128)} %param.9) | copy-start | bytes 196612

commit v3 on v2

v3 whole, which is shorter than its diff:
```python
import jax
import jax.numpy as jnp
from jax import lax
from jax.experimental import pallas as pl
from jax.experimental.pallas import tpu as pltpu
from jax.sharding import Mesh
from jax.sharding import PartitionSpec as P

ROW = ("x", "z")
COL = "col"


def contract(a, b, da, db):
    return lax.dot_general(a, b, (((da,), (db,)), ((), ())), preferred_element_type=jnp.float32)


def summed_over_x(parts):
    parts = lax.all_to_all(parts, "x", 0, 0)
    total = parts[0].astype(jnp.float32)
    for k in range(1, parts.shape[0]):
        total += parts[k].astype(jnp.float32)
    return total.astype(jnp.bfloat16)


def pack(left_ref, own_ref, out_ref):
    rows = left_ref.shape[0]
    cols = own_ref.shape[1]
    out_ref[0, :rows] = left_ref[...]
    out_ref[0, rows:, :cols] = own_ref[...]
    out_ref[0, rows:, cols:] = jnp.zeros((own_ref.shape[0], out_ref.shape[2] - cols), out_ref.dtype)


def packed(left_root, inputs, n):
    rows, order = left_root.shape
    wide, share, cols = order // n, inputs.shape[0] // n, inputs.shape[1]
    return pl.pallas_call(
        pack,
        grid=(n,),
        in_specs=[pl.BlockSpec((rows, wide), lambda x: (0, x)), pl.BlockSpec((share, cols), lambda x: (x, 0))],
        out_specs=pl.BlockSpec((1, rows + share, wide), lambda x: (x, 0, 0)),
        out_shape=jax.ShapeDtypeStruct((n, rows + share, wide), left_root.dtype),
    )(left_root, inputs)


def body(out_grad, inputs, left_root, right_root, momentum):
    nx, nz = lax.axis_size("x"), lax.axis_size("z")
    rows, order = left_root.shape
    cols = inputs.shape[1]
    wide = order // nx
    share = rows // nx

    got = lax.all_to_all(packed(left_root, inputs, nx), "x", 0, 0)
    left = got[:, :rows].reshape(nx * rows, wide)

    cotangent = lax.all_gather(out_grad.T, "z", axis=0).reshape(wide, -1)

    own = jnp.broadcast_to(got[:, rows:, :cols].reshape(rows, cols), (nz, rows, cols))
    part = contract(cotangent, left, 0, 1).astype(jnp.bfloat16)
    part = part.reshape(-1, nx, share, nx * rows).transpose(1, 0, 2, 3).reshape(nx, -1, nx * rows)
    part, own = lax.optimization_barrier((part, own))
    product = summed_over_x(part)

    tokens = lax.all_to_all(own, "z", 0, 0)
    tokens = tokens.reshape(nz, nx, share, cols).transpose(1, 0, 2, 3).reshape(-1, cols)
    panel = lax.all_gather(product, COL, axis=0, tiled=True)

    part = contract(panel, tokens, 0, 0).astype(jnp.bfloat16).reshape(nx, rows, cols)
    first = summed_over_x(part)
    panel = lax.all_gather(first, COL, axis=0)
    panel = panel.transpose(1, 0, 2).reshape(rows, -1)
    shaped = contract(panel, right_root, 1, 0)
    momentum_new = 0.9 * momentum + shaped
    update = (0.25 * (0.9 * momentum_new + shaped)).astype(jnp.bfloat16)
    return (momentum_new, update)


def solution(mesh):
    split = Mesh(mesh.devices.reshape(4, 16, mesh.shape["col"]), ("x", "z", "col"))
    in_specs = (P("col", ROW), P(ROW, "col"), P(ROW, None), P(None, "col"), P(ROW, "col"))
    out_specs = (P(ROW, "col"), P(ROW, "col"))
    return jax.shard_map(body, mesh=split, in_specs=in_specs, out_specs=out_specs, check_vma=False)
```

time: 121 us -> 120 us (level)
  blocking collectives: 96.1 us -> 104 us
  waiting for transfers between devices: 4.82 us -> 0.01 us
  starting transfers between devices: 12.5 us -> 8.82 us
  Pallas kernels: 0 us -> 3.31 us
  local copies, waits for them, and re-layouts: 3.73 us -> 0.98 us
    all_to_all x1 -> x2, blocking collectives: 7.21 us -> 15.6 us  [summed_over_x(): parts = lax.all_to_all(parts, 'x', 0, 0)]
    all_to_all x2 -> x1, waiting for transfers between devices: 4.82 us -> 0.01 us  [body(): got = lax.all_to_all(packed(left_root, inputs, nx), 'x', 0, 0)]
    all_to_all x2 -> x1, starting transfers between devices: 8.63 us -> 4.83 us  [body(): got = lax.all_to_all(packed(left_root, inputs, nx), 'x', 0, 0)]
    pallas_call x0 -> x1, Pallas kernels: none -> 3.31 us  [packed(): pl.pallas_call(pack, grid=(n,), in_specs=[pl.BlockSpec((rows, wide), lamb...]
    slice x2 -> x1, local copies, waits for them, and re-layouts: 2.09 us -> 0.01 us  [body(): got[:, rows:, :cols].reshape(rows, cols)]
  transfers between devices with their start and end apart: 3 -> 2, of which waited for: 1 -> 0; matrix products, arithmetic and copies ran while one was open for 0% -> 0% of each run, Pallas kernels for 0% -> 0%
where the time goes in v3:
time: 120 us
  blocking collectives  104 us (87%)
  starting transfers between devices  8.82 us (7%)
  Pallas kernels  3.31 us (3%)
  matrix products  1.81 us (2%)
    all_gather x1, blocking collectives, body(): cotangent = lax.all_gather(out_grad.T, 'z', axis=0).reshape(wide, -1)  38.9 us
    all_gather x1, blocking collectives, body(): panel = lax.all_gather(product, COL, axis=0, tiled=True)  28.3 us
    all_gather x1, blocking collectives, body(): panel = lax.all_gather(first, COL, axis=0)  21 us
    all_to_all x2, blocking collectives, summed_over_x(): parts = lax.all_to_all(parts, 'x', 0, 0)  15.6 us
    all_to_all x1, starting transfers between devices, body(): got = lax.all_to_all(packed(left_root, inputs, nx), 'x', 0, 0)  4.83 us
    all_to_all x1, starting transfers between devices, body(): tokens = lax.all_to_all(own, 'z', 0, 0)  3.99 us
    pallas_call x1, Pallas kernels, packed(): pl.pallas_call(pack, grid=(n,), in_specs=[pl.BlockSpec((rows, wide), lamb...  3.31 us
  transfers between devices with their start and end apart: 2, of which 0 were waited for; matrix products, arithmetic and copies ran while one was open for 0% of the time, Pallas kernels for 0%

profile of v3, /device:TPU:1, one launch (start us, length us, event | category | flops | bytes accessed | tf_op | source)
XLA Modules:
  0.0 119.6 jit_solution(4516904572650360851)
XLA Ops:
  0.6 0.0 copy-start
  0.6 0.0 copy-start.2
  0.7 3.3 %shard_map.68 = bf16[4,80,1024]{2,1,0:T(8,128)(2,1)} custom-call(bf16[64,4096]{1,0:T(8,128)(2,1)} %left_ref.1, bf16[64,256]{1,0:T(8,128)(2,1)} %own_ref.1), custom_call_target="tpu_custom_call" | custom-call | tf_op jit(solution)/shard_map/pallas_call | solution.py:36
  4.0 4.8 %all-to-all-start = ((bf16[4,80,1024]{2,1,0:T(8,128)(2,1)}), bf16[4,80,1024]{2,1,0:T(8,128)(2,1)S(1)}, u32[]{:S(2)}, u32[]{:S(2)}) async-start(bf16[4,80,1024]{2,1,0:T(8,128)(2,1)} %shard_map.68), calls=%async_computation | async-start | bytes 1310720 | tf_op jit(solution)/shard_map/all_to_all | solution.py:52
  8.8 0.0 copy-done.2
  8.8 38.9 %all-gather = bf16[1024,256]{1,0:T(8,128)(2,1)S(1)} all-gather(bf16[64,256]{1,0:T(8,128)(2,1)S(1)} %bitcast.34), channel_id=2, replica_groups=mesh['x'=4,'z'=16,'col'=16] {'z'}, dimensions={0}, use_global_device_ids=true | all-gather | bytes 557056 | tf_op jit(solution)/shard_map/all_gather | solution.py:55
  47.7 0.0 all-to-all-done
  47.8 0.3 convolution_convert_fusion.1
  48.2 0.8 broadcast_in_dim.3
  49.0 8.4 %all_to_all.20 = bf16[4,64,256]{2,1,0:T(8,128)(2,1)S(1)} all-to-all(bf16[4,64,256]{2,1,0:T(8,128)(2,1)S(1)} %bitcast.31), channel_id=1, replica_groups=mesh['x'=4,'z'=16,'col'=16] {'x'}, dimensions={0} | all-to-all | bytes 262144 | tf_op jit(solution)/shard_map/all_to_all | solution.py:18
  57.4 4.0 %all-to-all-start.2 = ((bf16[16,64,256]{2,1,0:T(8,128)(2,1)}), bf16[16,64,256]{2,1,0:T(8,128)(2,1)S(1)}, u32[]{:S(2)}, u32[]{:S(2)}) async-start(bf16[16,64,256]{2,1,0:T(8,128)(2,1)} %broadcast_in_dim.3), calls=%async_computation.2 | async-start | bytes 1048576 | tf_op jit(solution)/shard_map/all_to_all | solution.py:63
  61.4 28.3 %all-gather.1 = bf16[1,1024,256]{2,1,0:T(8,128)(2,1)S(1)} all-gather(bf16[1,64,256]{2,1,0:T(8,128)(2,1)S(1)} %add_convert_fusion.1), channel_id=3, replica_groups=mesh['x'=4,'z'=16,'col'=16] {'col'}, dimensions={1}, use_global_device_ids=true | all-gather | bytes 557056 | tf_op jit(solution)/shard_map/all_gather | solution.py:65
  89.8 0.0 all-to-all-done.2
  89.8 0.0 copy-start.1
  89.8 0.3 convolution_convert_fusion
  90.2 7.2 %all_to_all.21 = bf16[4,64,256]{2,1,0:T(8,128)(2,1)S(1)} all-to-all(bf16[4,64,256]{2,1,0:T(8,128)(2,1)S(1)} %bitcast.33), channel_id=1, replica_groups=mesh['x'=4,'z'=16,'col'=16] {'x'}, dimensions={0} | all-to-all | bytes 262144 | tf_op jit(solution)/shard_map/all_to_all | solution.py:18
  97.4 21.0 %all_gather.16 = bf16[16,64,256]{2,1,0:T(8,128)(2,1)S(1)} all-gather(bf16[1,64,256]{2,1,0:T(8,128)(2,1)S(1)} %add_convert_fusion), channel_id=1, replica_groups=mesh['x'=4,'z'=16,'col'=16] {'col'}, dimensions={0}, use_global_device_ids=true | all-gather | bytes 557056 | tf_op jit(solution)/shard_map/all_gather | solution.py:69
  118.5 0.0 copy-done
  118.5 0.0 copy-done.1
  118.5 1.1 multiply_convert_fusion
  (7 shorter events, 0.2 us)
Async XLA Ops:
  0.6 117.9 %copy-start = (bf16[4096,256]{1,0:T(8,128)(2,1)S(1)}, bf16[4096,256]{1,0:T(8,128)(2,1)}, u32[]{:S(2)}) copy-start(bf16[4096,256]{1,0:T(8,128)(2,1)} %param.8) | copy-start | bytes 6291460
  0.6 8.2 %copy-start.2 = (bf16[256,64]{0,1:T(8,128)(2,1)S(1)}, bf16[256,64]{0,1:T(8,128)(2,1)}, u32[]{:S(2)}) copy-start(bf16[256,64]{0,1:T(8,128)(2,1)} %param.5) | copy-start | bytes 98308
  4.0 43.8 %all-to-all-start = ((bf16[4,80,1024]{2,1,0:T(8,128)(2,1)}), bf16[4,80,1024]{2,1,0:T(8,128)(2,1)S(1)}, u32[]{:S(2)}, u32[]{:S(2)}) async-start(bf16[4,80,1024]{2,1,0:T(8,128)(2,1)} %shard_map.68), calls=%async_computation | async-start | bytes 1310720 | tf_op jit(solution)/shard_map/all_to_all | solution.py:52
  57.4 32.4 %all-to-all-start.2 = ((bf16[16,64,256]{2,1,0:T(8,128)(2,1)}), bf16[16,64,256]{2,1,0:T(8,128)(2,1)S(1)}, u32[]{:S(2)}, u32[]{:S(2)}) async-start(bf16[16,64,256]{2,1,0:T(8,128)(2,1)} %broadcast_in_dim.3), calls=%async_computation.2 | async-start | bytes 1048576 | tf_op jit(solution)/shard_map/all_to_all | solution.py:63
  89.8 28.7 %copy-start.1 = (f32[64,256]{1,0:T(8,128)S(1)}, f32[64,256]{1,0:T(8,128)}, u32[]{:S(2)}) copy-start(f32[64,256]{1,0:T(8,128)} %param.9) | copy-start | bytes 196612

commit v4 on v3

v4 whole, which is shorter than its diff:
```python
import jax
import jax.numpy as jnp
from jax import lax
from jax.experimental import pallas as pl
from jax.experimental.pallas import tpu as pltpu
from jax.sharding import Mesh
from jax.sharding import PartitionSpec as P


ROW = ("x", "z")
COL = "col"


def contract(a, b, da, db):
    return lax.dot_general(a, b, (((da,), (db,)), ((), ())), preferred_element_type=jnp.float32)


def summed_over_x(parts):
    parts = lax.all_to_all(parts, "x", 0, 0)
    total = parts[0].astype(jnp.float32)
    for k in range(1, parts.shape[0]):
        total += parts[k].astype(jnp.float32)
    return total.astype(jnp.bfloat16)


def summed_by_permutes(parts):
    n = parts.shape[0]
    me = lax.axis_index("x")
    total = lax.dynamic_index_in_dim(parts, me, 0, False).astype(jnp.float32)
    for k in range(1, n):
        sent = lax.dynamic_index_in_dim(parts, lax.rem(me + k, n), 0, False)
        total += lax.ppermute(sent, "x", [(x, (x + k) % n) for x in range(n)]).astype(jnp.float32)
    return total.astype(jnp.bfloat16)


def pack(left_ref, own_ref, out_ref, held, fetched, stored):
    n, _, wide = held.shape
    rows = left_ref.shape[0]
    share, cols = own_ref.shape[0] // n, own_ref.shape[1]
    fetches = []
    for x in range(n):
        for k, (source, target) in enumerate(
            (
                (left_ref.at[:, pl.ds(x * wide, wide)], held.at[x, pl.ds(0, rows)]),
                (own_ref.at[pl.ds(x * share, share)], held.at[x, pl.ds(rows, share), pl.ds(0, cols)]),
            )
        ):
            copy = pltpu.make_async_copy(source, target, fetched.at[x, k])
            copy.start()
            fetches.append(copy)
    held[:, rows:, cols:] = jnp.zeros((n, share, wide - cols), held.dtype)
    stores = []
    for x in range(n):
        fetches[2 * x].wait()
        fetches[2 * x + 1].wait()
        copy = pltpu.make_async_copy(held.at[x], out_ref.at[x], stored.at[x])
        copy.start()
        stores.append(copy)
    for copy in stores:
        copy.wait()


def packed(left_root, inputs, n):
    rows, order = left_root.shape
    shape = (n, rows + inputs.shape[0] // n, order // n)
    return pl.pallas_call(
        pack,
        in_specs=[pl.BlockSpec(memory_space=pl.ANY)] * 2,
        out_specs=pl.BlockSpec(memory_space=pl.ANY),
        out_shape=jax.ShapeDtypeStruct(shape, left_root.dtype),
        scratch_shapes=[
            pltpu.VMEM(shape, left_root.dtype),
            pltpu.SemaphoreType.DMA((n, 2)),
            pltpu.SemaphoreType.DMA((n,)),
        ],
    )(left_root, inputs)


def body(out_grad, inputs, left_root, right_root, momentum):
    nx, nz = lax.axis_size("x"), lax.axis_size("z")
    rows, order = left_root.shape
    cols = inputs.shape[1]
    wide = order // nx
    share = rows // nx

    blocks = packed(left_root, inputs, nx)
    got = lax.all_to_all(blocks, "x", 0, 0)
    left = got[:, :rows].reshape(nx * rows, wide)

    cotangent = lax.all_gather(out_grad.T, "z", axis=0, tiled=True)

    own = jnp.broadcast_to(got[:, rows:, :cols].reshape(rows, cols), (nz, rows, cols))
    part = contract(cotangent, left, 0, 1).astype(jnp.bfloat16)
    part = part.reshape(-1, nx, share, nx * rows).transpose(1, 0, 2, 3).reshape(nx, -1, nx * rows)
    product = summed_by_permutes(part)

    tokens = lax.all_to_all(own, "z", 0, 0)
    tokens = tokens.reshape(nz, nx, share, cols).transpose(1, 0, 2, 3).reshape(-1, cols)
    panel = lax.all_gather(product, COL, axis=0, tiled=True)

    part = contract(panel, tokens, 0, 0).astype(jnp.bfloat16).reshape(nx, rows, cols)
    first = summed_over_x(part)
    panel = lax.all_gather(first, COL, axis=0)
    panel = panel.transpose(1, 0, 2).reshape(rows, -1)
    shaped = contract(panel, right_root, 1, 0)
    momentum_new = 0.9 * momentum + shaped
    update = (0.25 * (0.9 * momentum_new + shaped)).astype(jnp.bfloat16)
    return (momentum_new, update)


def solution(mesh):
    split = Mesh(mesh.devices.reshape(4, 16, mesh.shape["col"]), ("x", "z", "col"))
    in_specs = (P("col", ROW), P(ROW, "col"), P(ROW, None), P(None, "col"), P(ROW, "col"))
    out_specs = (P(ROW, "col"), P(ROW, "col"))

    def step(*args):
        return body(*args)

    step = jax.shard_map(step, mesh=split, in_specs=in_specs, out_specs=out_specs, check_vma=False)
    return step
```

time: 120 us -> 149 us (1.24)
  starting transfers between devices: 8.82 us -> 28.8 us
  blocking collectives: 104 us -> 110 us
  waiting for transfers between devices: 0.01 us -> 3.94 us
    all_to_all x1, starting transfers between devices: 3.99 us -> 21 us  [body(): tokens = lax.all_to_all(own, 'z', 0, 0)]
    all_to_all x0 -> x1, blocking collectives: none -> 12.5 us  [body(): got = lax.all_to_all(blocks, 'x', 0, 0)]
    all_to_all x2 -> x1, blocking collectives: 15.6 us -> 7.32 us  [summed_over_x(): parts = lax.all_to_all(parts, 'x', 0, 0)]
    ppermute x0 -> x3, starting transfers between devices: none -> 7.81 us  [summed_by_permutes(): lax.ppermute(sent, 'x', [(x, (x + k) % n) for x in range(n)])]
    all_gather x1, blocking collectives: 38.9 us -> 45.8 us  [body(): cotangent = lax.all_gather(out_grad.T, 'z', axis=0, tiled=True)]
    all_to_all x1 -> x0, starting transfers between devices: 4.83 us -> none  [body(): got = lax.all_to_all(packed(left_root, inputs, nx), 'x', 0, 0)]
    ppermute x0 -> x3, waiting for transfers between devices: none -> 3.93 us  [summed_by_permutes(): lax.ppermute(sent, 'x', [(x, (x + k) % n) for x in range(n)])]
    all_gather x1, blocking collectives: 21 us -> 17.5 us  [body(): panel = lax.all_gather(first, COL, axis=0)]
  transfers between devices with their start and end apart: 2 -> 4, of which waited for: 0 -> 2; matrix products, arithmetic and copies ran while one was open for 0% -> 0% of each run, Pallas kernels for 0% -> 0%
where the time goes in v4:
time: 149 us
  blocking collectives  110 us (74%)
  starting transfers between devices  28.8 us (19%)
  waiting for transfers between devices  3.94 us (3%)
  Pallas kernels  2.06 us (1%)
  matrix products  1.79 us (1%)
    all_gather x1, blocking collectives, body(): cotangent = lax.all_gather(out_grad.T, 'z', axis=0, tiled=True)  45.8 us
    all_gather x1, blocking collectives, body(): panel = lax.all_gather(product, COL, axis=0, tiled=True)  27 us
    all_to_all x1, starting transfers between devices, body(): tokens = lax.all_to_all(own, 'z', 0, 0)  21 us
    all_gather x1, blocking collectives, body(): panel = lax.all_gather(first, COL, axis=0)  17.5 us
    all_to_all x1, blocking collectives, body(): got = lax.all_to_all(blocks, 'x', 0, 0)  12.5 us
    ppermute x3, starting transfers between devices, summed_by_permutes(): lax.ppermute(sent, 'x', [(x, (x + k) % n) for x in range(n)])  7.81 us
    all_to_all x1, blocking collectives, summed_over_x(): parts = lax.all_to_all(parts, 'x', 0, 0)  7.32 us
    ppermute x3, waiting for transfers between devices, summed_by_permutes(): lax.ppermute(sent, 'x', [(x, (x + k) % n) for x in range(n)])  3.93 us
  transfers between devices with their start and end apart: 4, of which 2 were waited for; matrix products, arithmetic and copies ran while one was open for 0% of the time, Pallas kernels for 0%

profile of v4, /device:TPU:1, one launch (start us, length us, event | category | flops | bytes accessed | tf_op | source)
XLA Modules:
  0.0 148.6 jit_solution(7335724149105209450)
XLA Ops:
  0.6 0.0 copy-start
  0.6 0.0 copy-start.2
  0.7 2.1 %shard_map.68 = bf16[4,80,1024]{2,1,0:T(8,128)(2,1)} custom-call(bf16[64,4096]{1,0:T(8,128)(2,1)} %left_ref.1, bf16[64,256]{1,0:T(8,128)(2,1)} %own_ref.1), custom_call_target="tpu_custom_call" | custom-call | tf_op jit(solution)/shard_map/pallas_call | solution.py:66
  2.7 12.5 %all_to_all.15 = bf16[4,80,1024]{2,1,0:T(8,128)(2,1)S(1)} all-to-all(bf16[4,80,1024]{2,1,0:T(8,128)(2,1)} %shard_map.68), channel_id=1, replica_groups=mesh['x'=4,'z'=16,'col'=16] {'x'}, dimensions={0} | all-to-all | bytes 1310720 | tf_op jit(solution)/shard_map/all_to_all | solution.py:87
  15.2 0.9 broadcast_in_dim.3
  16.1 21.0 %all-to-all-start.1 = ((bf16[16,64,256]{2,1,0:T(8,128)(2,1)}), bf16[16,64,256]{2,1,0:T(8,128)(2,1)S(1)}, u32[]{:S(2)}, u32[]{:S(2)}) async-start(bf16[16,64,256]{2,1,0:T(8,128)(2,1)} %broadcast_in_dim.3), calls=%async_computation.1 | async-start | bytes 1048576 | tf_op jit(solution)/shard_map/all_to_all | solution.py:97
  37.1 0.0 copy-done.2
  37.1 45.8 %all_gather.10 = bf16[1024,256]{1,0:T(8,128)(2,1)S(1)} all-gather(bf16[64,256]{1,0:T(8,128)(2,1)S(1)} %bitcast.42), channel_id=1, replica_groups=mesh['x'=4,'z'=16,'col'=16] {'z'}, dimensions={0}, use_global_device_ids=true | all-gather | bytes 557056 | tf_op jit(solution)/shard_map/all_gather | solution.py:90
  82.9 0.4 convolution_convert_fusion.1
  83.3 2.8 %collective-permute-start.2 = (bf16[64,256]{1,0:T(8,128)(2,1)S(1)}, bf16[64,256]{1,0:T(8,128)(2,1)S(1)}, u32[]{:S(2)}, u32[]{:S(2)}) collective-permute-start(bf16[64,256]{1,0:T(8,128)(2,1)S(1)} %get-tuple-element.5), channel_id=1, source_target_pairs={{0,768},{256,0},{512,256},{768,512},{1,769},{257,1},{513,257},{769... | collective-permute-start | bytes 98312 | tf_op jit(solution)/shard_map/ppermute | solution.py:32
  86.1 3.1 %collective-permute-start.1 = (bf16[64,256]{1,0:T(8,128)(2,1)S(1)}, bf16[64,256]{1,0:T(8,128)(2,1)S(1)}, u32[]{:S(2)}, u32[]{:S(2)}) collective-permute-start(bf16[64,256]{1,0:T(8,128)(2,1)S(1)} %get-tuple-element.6), channel_id=1, source_target_pairs={{0,512},{256,768},{512,0},{768,256},{1,513},{257,769},{513,1},{769... | collective-permute-start | bytes 98312 | tf_op jit(solution)/shard_map/ppermute | solution.py:32
  89.2 1.9 %collective-permute-start = (bf16[64,256]{1,0:T(8,128)(2,1)S(1)}, bf16[64,256]{1,0:T(8,128)(2,1)S(1)}, u32[]{:S(2)}, u32[]{:S(2)}) collective-permute-start(bf16[64,256]{1,0:T(8,128)(2,1)S(1)} %get-tuple-element.4), channel_id=1, source_target_pairs={{0,256},{256,512},{512,768},{768,0},{1,257},{257,513},{513,769},{7... | collective-permute-start | bytes 98312 | tf_op jit(solution)/shard_map/ppermute | solution.py:32
  91.2 0.0 collective-permute-done.2
  91.2 1.1 collective-permute-done.1
  92.3 2.8 %collective-permute-done = bf16[64,256]{1,0:T(8,128)(2,1)S(1)} collective-permute-done((bf16[64,256]{1,0:T(8,128)(2,1)S(1)}, bf16[64,256]{1,0:T(8,128)(2,1)S(1)}, u32[]{:S(2)}, u32[]{:S(2)}) %collective-permute-start) | collective-permute-done | bytes 32800 | tf_op jit(solution)/shard_map/ppermute | solution.py:32
  95.1 27.0 %all_gather.11 = bf16[1024,256]{1,0:T(8,128)(2,1)S(1)} all-gather(bf16[64,256]{1,0:T(8,128)(2,1)S(1)} %fusion.2), channel_id=1, replica_groups=mesh['x'=4,'z'=16,'col'=16] {'col'}, dimensions={0}, use_global_device_ids=true | all-gather | bytes 557056 | tf_op jit(solution)/shard_map/all_gather | solution.py:99
  122.2 0.0 all-to-all-done.1
  122.2 0.0 copy-start.1
  122.2 0.3 convolution_convert_fusion
  122.6 7.3 %all_to_all.16 = bf16[4,64,256]{2,1,0:T(8,128)(2,1)S(1)} all-to-all(bf16[4,64,256]{2,1,0:T(8,128)(2,1)S(1)} %bitcast.41), channel_id=1, replica_groups=mesh['x'=4,'z'=16,'col'=16] {'x'}, dimensions={0} | all-to-all | bytes 262144 | tf_op jit(solution)/shard_map/all_to_all | solution.py:19
  129.9 17.5 %all_gather.12 = bf16[16,64,256]{2,1,0:T(8,128)(2,1)S(1)} all-gather(bf16[1,64,256]{2,1,0:T(8,128)(2,1)S(1)} %add_convert_fusion), channel_id=1, replica_groups=mesh['x'=4,'z'=16,'col'=16] {'col'}, dimensions={0}, use_global_device_ids=true | all-gather | bytes 557056 | tf_op jit(solution)/shard_map/all_gather | solution.py:103
  147.5 0.0 copy-done
  147.5 0.0 copy-done.1
  147.5 1.1 multiply_convert_fusion
  (8 shorter events, 0.2 us)
Async XLA Ops:
  0.6 146.8 %copy-start = (bf16[4096,256]{1,0:T(8,128)(2,1)S(1)}, bf16[4096,256]{1,0:T(8,128)(2,1)}, u32[]{:S(2)}) copy-start(bf16[4096,256]{1,0:T(8,128)(2,1)} %param.8) | copy-start | bytes 6291460
  0.6 36.4 %copy-start.2 = (bf16[256,64]{0,1:T(8,128)(2,1)S(1)}, bf16[256,64]{0,1:T(8,128)(2,1)}, u32[]{:S(2)}) copy-start(bf16[256,64]{0,1:T(8,128)(2,1)} %param.5) | copy-start | bytes 98308
  16.1 106.1 %all-to-all-start.1 = ((bf16[16,64,256]{2,1,0:T(8,128)(2,1)}), bf16[16,64,256]{2,1,0:T(8,128)(2,1)S(1)}, u32[]{:S(2)}, u32[]{:S(2)}) async-start(bf16[16,64,256]{2,1,0:T(8,128)(2,1)} %broadcast_in_dim.3), calls=%async_computation.1 | async-start | bytes 1048576 | tf_op jit(solution)/shard_map/all_to_all | solution.py:97
  83.3 7.8 %collective-permute-start.2 = (bf16[64,256]{1,0:T(8,128)(2,1)S(1)}, bf16[64,256]{1,0:T(8,128)(2,1)S(1)}, u32[]{:S(2)}, u32[]{:S(2)}) collective-permute-start(bf16[64,256]{1,0:T(8,128)(2,1)S(1)} %get-tuple-element.5), channel_id=1, source_target_pairs={{0,768},{256,0},{512,256},{768,512},{1,769},{257,1},{513,257},{769... | collective-permute-start | bytes 98312 | tf_op jit(solution)/shard_map/ppermute | solution.py:32
  86.1 6.2 %collective-permute-start.1 = (bf16[64,256]{1,0:T(8,128)(2,1)S(1)}, bf16[64,256]{1,0:T(8,128)(2,1)S(1)}, u32[]{:S(2)}, u32[]{:S(2)}) collective-permute-start(bf16[64,256]{1,0:T(8,128)(2,1)S(1)} %get-tuple-element.6), channel_id=1, source_target_pairs={{0,512},{256,768},{512,0},{768,256},{1,513},{257,769},{513,1},{769... | collective-permute-start | bytes 98312 | tf_op jit(solution)/shard_map/ppermute | solution.py:32
  89.2 5.9 %collective-permute-start = (bf16[64,256]{1,0:T(8,128)(2,1)S(1)}, bf16[64,256]{1,0:T(8,128)(2,1)S(1)}, u32[]{:S(2)}, u32[]{:S(2)}) collective-permute-start(bf16[64,256]{1,0:T(8,128)(2,1)S(1)} %get-tuple-element.4), channel_id=1, source_target_pairs={{0,256},{256,512},{512,768},{768,0},{1,257},{257,513},{513,769},{7... | collective-permute-start | bytes 98312 | tf_op jit(solution)/shard_map/ppermute | solution.py:32
  122.2 25.3 %copy-start.1 = (f32[64,256]{1,0:T(8,128)S(1)}, f32[64,256]{1,0:T(8,128)}, u32[]{:S(2)}) copy-start(f32[64,256]{1,0:T(8,128)} %param.9) | copy-start | bytes 196612

commit v5 on v3

v5 whole, which is shorter than its diff:
```python
import jax
import jax.numpy as jnp
from jax import lax
from jax.experimental import pallas as pl
from jax.experimental.pallas import tpu as pltpu
from jax.sharding import Mesh
from jax.sharding import PartitionSpec as P

ROW = ("x", "z")
COL = "col"


def contract(a, b, da, db):
    return lax.dot_general(a, b, (((da,), (db,)), ((), ())), preferred_element_type=jnp.float32)


def summed_over_x(parts):
    parts = lax.all_to_all(parts, "x", 0, 0)
    total = parts[0].astype(jnp.float32)
    for k in range(1, parts.shape[0]):
        total += parts[k].astype(jnp.float32)
    return total


def pack(place_ref, left_ref, own_ref, out_ref, held, fetched, stored):
    n, copies, both, cols = out_ref.shape
    share = both // 2
    wide = left_ref.shape[1] // n
    across = wide // cols
    down = pl.multiple_of(place_ref[0] // across * share, share)
    right = place_ref[0] % across * cols
    fetches = []
    for x in range(n):
        left = left_ref.at[pl.ds(down, share), pl.ds(pl.multiple_of(x * wide + right, cols), cols)]
        own = own_ref.at[pl.ds(x * share, share)]
        for k, source in enumerate((left, own)):
            copy = pltpu.make_async_copy(source, held.at[x, pl.ds(k * share, share)], fetched.at[x, k])
            copy.start()
            fetches.append(copy)
    stores = []
    for x in range(n):
        fetches[2 * x].wait()
        fetches[2 * x + 1].wait()
        for c in range(copies):
            copy = pltpu.make_async_copy(held.at[x], out_ref.at[x, c], stored.at[x, c])
            copy.start()
            stores.append(copy)
    for copy in stores:
        copy.wait()


def packed(left_root, inputs, n, copies):
    share, cols = inputs.shape[0] // n, inputs.shape[1]
    return pl.pallas_call(
        pack,
        in_specs=[
            pl.BlockSpec(memory_space=pltpu.SMEM),
            pl.BlockSpec(memory_space=pl.ANY),
            pl.BlockSpec(memory_space=pl.ANY),
        ],
        out_specs=pl.BlockSpec(memory_space=pl.ANY),
        out_shape=jax.ShapeDtypeStruct((n, copies, 2 * share, cols), inputs.dtype),
        scratch_shapes=[
            pltpu.VMEM((n, 2 * share, cols), inputs.dtype),
            pltpu.SemaphoreType.DMA((n, 2)),
            pltpu.SemaphoreType.DMA((n, copies)),
        ],
    )(lax.axis_index(COL).astype(jnp.int32)[None], left_root, inputs)


def body(out_grad, inputs, left_root, right_root, momentum):
    nx, nz, nc = lax.axis_size("x"), lax.axis_size("z"), lax.axis_size(COL)
    rows, order = left_root.shape
    cols = inputs.shape[1]
    wide = order // nx
    share = rows // nx

    blocks = packed(left_root, inputs, nx, nc).reshape(nx * nc, 2 * share, cols)
    with jax.named_scope("turn"):
        got = lax.all_to_all(blocks, ("x", COL), 0, 0)
    left = got[:, :share].reshape(nx, rows // share, wide // cols, share, cols)
    left = left.transpose(0, 1, 3, 2, 4).reshape(nx * rows, wide)
    own = got[:, share:].reshape(nx, nc, share, cols).transpose(0, 2, 1, 3).reshape(rows, -1)

    with jax.named_scope("cotangent"):
        cotangent = lax.all_gather(out_grad.T, "z", axis=0, tiled=True)

    part = contract(cotangent, left, 0, 1).astype(jnp.bfloat16)
    part = part.reshape(-1, nx, share, nx * rows).transpose(1, 0, 2, 3).reshape(nx, -1, nx * rows)
    product = summed_over_x(part).astype(jnp.bfloat16)

    own = contract(own, right_root, 1, 0).astype(jnp.bfloat16)
    own = jnp.broadcast_to(own, (nz, rows, cols))
    tokens = lax.all_to_all(own, "z", 0, 0)
    tokens = tokens.reshape(nz, nx, share, cols).transpose(1, 0, 2, 3).reshape(-1, cols)
    panel = lax.all_gather(product, COL, axis=0, tiled=True)

    part = contract(panel, tokens, 0, 0).astype(jnp.bfloat16).reshape(nx, rows, cols)
    shaped = summed_over_x(part)
    momentum_new = 0.9 * momentum + shaped
    update = (0.25 * (0.9 * momentum_new + shaped)).astype(jnp.bfloat16)
    return (momentum_new, update)


def solution(mesh):
    split = Mesh(mesh.devices.reshape(4, 16, mesh.shape["col"]), ("x", "z", "col"))
    in_specs = (P("col", ROW), P(ROW, "col"), P(ROW, None), P(None, "col"), P(ROW, "col"))
    out_specs = (P(ROW, "col"), P(ROW, "col"))
    return jax.shard_map(body, mesh=split, in_specs=in_specs, out_specs=out_specs, check_vma=False)
```

time: 120 us -> 111 us (0.925)
  the two profiles are of different devices: /device:TPU:1 before, /device:TPU:2 now
where the time goes in v5:
time: 111 us
  blocking collectives  67.6 us (61%)
  starting transfers between devices  26.2 us (24%)
  waiting for transfers between devices  8.64 us (8%)
  local copies, waits for them, and re-layouts  3.17 us (3%)
  Pallas kernels  2.48 us (2%)
  matrix products  1.16 us (1%)
    all_gather x1, blocking collectives, body(): cotangent = lax.all_gather(out_grad.T, 'z', axis=0, tiled=True)  40.9 us
    all_gather x1, blocking collectives, body(): panel = lax.all_gather(product, COL, axis=0, tiled=True)  18.3 us
    all_to_all x1, starting transfers between devices, body(): got = lax.all_to_all(blocks, ('x', COL), 0, 0)  17.4 us
    all_to_all x1, blocking collectives, summed_over_x(): parts = lax.all_to_all(parts, 'x', 0, 0)  8.37 us
    all_to_all x1, waiting for transfers between devices, body(): tokens = lax.all_to_all(own, 'z', 0, 0)  4.95 us
    all_to_all x1, starting transfers between devices, summed_over_x(): parts = lax.all_to_all(parts, 'x', 0, 0)  4.89 us
    all_to_all x1, starting transfers between devices, body(): tokens = lax.all_to_all(own, 'z', 0, 0)  3.98 us
    all_to_all x1, waiting for transfers between devices, summed_over_x(): parts = lax.all_to_all(parts, 'x', 0, 0)  3.68 us
  transfers between devices with their start and end apart: 3, of which 2 were waited for; matrix products, arithmetic and copies ran while one was open for 1% of the time, Pallas kernels for 0%

profile of v5, /device:TPU:2, one launch (start us, length us, event | category | flops | bytes accessed | tf_op | source)
XLA Modules:
  0.0 110.7 jit_solution(18411999003814672435)
XLA Ops:
  0.6 0.0 copy-start
  0.6 0.0 copy-start.4
  0.7 2.5 %shard_map.68 = bf16[4,16,32,256]{3,2,1,0:T(8,128)(2,1)} custom-call(s32[1]{0:T(128)} %bitcast.place_ref, bf16[64,4096]{1,0:T(8,128)(2,1)} %left_ref.1, bf16[64,256]{1,0:T(8,128)(2,1)} %own_ref.1), custom_call_target="tpu_custom_call" | custom-call | tf_op jit(solution)/shard_map/pallas_call | solution.py:54
  3.1 17.4 %all-to-all-start = ((bf16[64,32,256]{2,1,0:T(8,128)(2,1)}), bf16[64,32,256]{2,1,0:T(8,128)(2,1)S(1)}, u32[]{:S(2)}, u32[]{:S(2)}) async-start(bf16[64,32,256]{2,1,0:T(8,128)(2,1)} %bitcast.42), calls=%async_computation | async-start | bytes 2097152 | tf_op jit(solution)/shard_map/turn/all_to_all | solution.py:80
  20.5 0.0 copy-done.4
  20.5 40.9 %all_gather.6 = bf16[1024,256]{1,0:T(8,128)(2,1)} all-gather(bf16[64,256]{1,0:T(8,128)(2,1)S(1)} %bitcast.53), channel_id=1, replica_groups=mesh['x'=4,'z'=16,'col'=16] {'z'}, dimensions={0}, use_global_device_ids=true | all-gather | bytes 557056 | tf_op jit(solution)/shard_map/cotangent/all_gather | solution.py:86
  61.4 0.0 all-to-all-done
  61.4 0.0 copy-start.1
  61.4 0.9 fusion.3
  62.3 0.0 copy-start.2
  62.3 0.3 copy.8
  62.6 0.1 copy.12
  62.7 0.0 copy-done.1
  62.7 0.4 convolution_convert_fusion.1
  63.0 0.7 copy.9
  63.7 4.9 %all-to-all-start.1 = ((bf16[4,64,256]{2,1,0:T(8,128)(2,1)}), bf16[4,64,256]{2,1,0:T(8,128)(2,1)S(1)}, u32[]{:S(2)}, u32[]{:S(2)}) async-start(bf16[4,64,256]{2,1,0:T(8,128)(2,1)} %bitcast.8), calls=%async_computation.1 | async-start | bytes 262144 | tf_op jit(solution)/shard_map/all_to_all | solution.py:18
  68.6 0.0 copy-done.2
  68.6 0.2 copy.10
  68.7 0.2 copy.13
  68.9 0.0 copy-done
  68.9 0.5 convolution_convert_fusion.2
  69.4 3.7 %all-to-all-done.1 = bf16[4,64,256]{2,1,0:T(8,128)(2,1)S(1)} async-done(((bf16[4,64,256]{2,1,0:T(8,128)(2,1)}), bf16[4,64,256]{2,1,0:T(8,128)(2,1)S(1)}, u32[]{:S(2)}, u32[]{:S(2)}) %all-to-all-start.1) | async-done | bytes 131104 | tf_op jit(solution)/shard_map/all_to_all | solution.py:18
  73.1 0.9 broadcast_in_dim.7
  74.0 0.0 copy-start.3
  74.0 4.0 %all-to-all-start.2 = ((bf16[16,64,256]{2,1,0:T(8,128)(2,1)}), bf16[16,64,256]{2,1,0:T(8,128)(2,1)S(1)}, u32[]{:S(2)}, u32[]{:S(2)}) async-start(bf16[16,64,256]{2,1,0:T(8,128)(2,1)} %broadcast_in_dim.7), calls=%async_computation.2 | async-start | bytes 1048576 | tf_op jit(solution)/shard_map/all_to_all | solution.py:94
  78.0 18.3 %all-gather = bf16[1,1024,256]{2,1,0:T(8,128)(2,1)S(1)} all-gather(bf16[1,64,256]{2,1,0:T(8,128)(2,1)S(1)} %add_convert_fusion), channel_id=2, replica_groups=mesh['x'=4,'z'=16,'col'=16] {'col'}, dimensions={1}, use_global_device_ids=true | all-gather | bytes 557056 | tf_op jit(solution)/shard_map/all_gather | solution.py:96
  96.3 4.9 %all-to-all-done.2 = bf16[16,64,256]{2,1,0:T(8,128)(2,1)S(1)} async-done(((bf16[16,64,256]{2,1,0:T(8,128)(2,1)}), bf16[16,64,256]{2,1,0:T(8,128)(2,1)S(1)}, u32[]{:S(2)}, u32[]{:S(2)}) %all-to-all-start.2) | async-done | bytes 524320 | tf_op jit(solution)/shard_map/all_to_all | solution.py:94
  101.3 0.3 convolution_convert_fusion
  101.6 8.4 %all_to_all.20 = bf16[4,64,256]{2,1,0:T(8,128)(2,1)S(1)} all-to-all(bf16[4,64,256]{2,1,0:T(8,128)(2,1)S(1)} %bitcast.52), channel_id=1, replica_groups=mesh['x'=4,'z'=16,'col'=16] {'x'}, dimensions={0} | all-to-all | bytes 262144 | tf_op jit(solution)/shard_map/all_to_all | solution.py:18
  110.0 0.0 copy-done.3
  110.0 0.7 fusion.2
  (2 shorter events, 0.1 us)
Async XLA Ops:
  0.6 68.3 %copy-start = (bf16[4096,256]{1,0:T(8,128)(2,1)S(1)}, bf16[4096,256]{1,0:T(8,128)(2,1)}, u32[]{:S(2)}) copy-start(bf16[4096,256]{1,0:T(8,128)(2,1)} %param.8) | copy-start | bytes 6291460
  0.6 19.9 %copy-start.4 = (bf16[256,64]{0,1:T(8,128)(2,1)S(1)}, bf16[256,64]{0,1:T(8,128)(2,1)}, u32[]{:S(2)}) copy-start(bf16[256,64]{0,1:T(8,128)(2,1)} %param.5) | copy-start | bytes 98308
  3.1 58.2 %all-to-all-start = ((bf16[64,32,256]{2,1,0:T(8,128)(2,1)}), bf16[64,32,256]{2,1,0:T(8,128)(2,1)S(1)}, u32[]{:S(2)}, u32[]{:S(2)}) async-start(bf16[64,32,256]{2,1,0:T(8,128)(2,1)} %bitcast.42), calls=%async_computation | async-start | bytes 2097152 | tf_op jit(solution)/shard_map/turn/all_to_all | solution.py:80
  61.4 1.3 %copy-start.1 = (bf16[1024,256]{1,0:T(8,128)(2,1)S(1)}, bf16[1024,256]{1,0:T(8,128)(2,1)}, u32[]{:S(2)}) copy-start(bf16[1024,256]{1,0:T(8,128)(2,1)} %all_gather.6) | copy-start | bytes 1572868
  62.3 6.3 %copy-start.2 = (bf16[64,16,256]{2,1,0:T(8,128)(2,1)S(1)}, bf16[64,16,256]{2,1,0:T(8,128)(2,1)}, u32[]{:S(2)}) copy-start(bf16[64,16,256]{2,1,0:T(8,128)(2,1)} %get-tuple-element.5) | copy-start | bytes 1572868
  63.7 9.4 %all-to-all-start.1 = ((bf16[4,64,256]{2,1,0:T(8,128)(2,1)}), bf16[4,64,256]{2,1,0:T(8,128)(2,1)S(1)}, u32[]{:S(2)}, u32[]{:S(2)}) async-start(bf16[4,64,256]{2,1,0:T(8,128)(2,1)} %bitcast.8), calls=%async_computation.1 | async-start | bytes 262144 | tf_op jit(solution)/shard_map/all_to_all | solution.py:18
  74.0 36.1 %copy-start.3 = (f32[64,256]{1,0:T(8,128)S(1)}, f32[64,256]{1,0:T(8,128)}, u32[]{:S(2)}) copy-start(f32[64,256]{1,0:T(8,128)} %param.9) | copy-start | bytes 196612
  74.0 27.3 %all-to-all-start.2 = ((bf16[16,64,256]{2,1,0:T(8,128)(2,1)}), bf16[16,64,256]{2,1,0:T(8,128)(2,1)S(1)}, u32[]{:S(2)}, u32[]{:S(2)}) async-start(bf16[16,64,256]{2,1,0:T(8,128)(2,1)} %broadcast_in_dim.7), calls=%async_computation.2 | async-start | bytes 1048576 | tf_op jit(solution)/shard_map/all_to_all | solution.py:94

commit v6 on v5

v6 whole, which is shorter than its diff:
```python
import jax
import jax.numpy as jnp
from jax import lax
from jax.experimental import pallas as pl
from jax.experimental.pallas import tpu as pltpu
from jax.sharding import Mesh
from jax.sharding import PartitionSpec as P


ROW = ("x", "z")
COL = ("y", "core")


def contract(a, b, da, db):
    return lax.dot_general(a, b, (((da,), (db,)), ((), ())), preferred_element_type=jnp.float32)


def summed_over_x(parts):
    parts = lax.all_to_all(parts, "x", 0, 0)
    total = parts[0].astype(jnp.float32)
    for k in range(1, parts.shape[0]):
        total += parts[k].astype(jnp.float32)
    return total


def pack(place_ref, left_ref, own_ref, out_ref, held, fetched, stored):
    n, copies, both, cols = out_ref.shape
    share = own_ref.shape[0] // n
    piece = both - share
    wide = left_ref.shape[1] // n
    across = wide // cols
    down = pl.multiple_of(place_ref[0] // across * piece, piece)
    right = place_ref[0] % across * cols
    fetches = []
    for x in range(n):
        left = left_ref.at[pl.ds(down, piece), pl.ds(pl.multiple_of(x * wide + right, cols), cols)]
        own = own_ref.at[pl.ds(x * share, share)]
        for k, (source, start) in enumerate(((left, 0), (own, piece))):
            copy = pltpu.make_async_copy(source, held.at[x, pl.ds(start, source.shape[0])], fetched.at[x, k])
            copy.start()
            fetches.append(copy)
    stores = []
    for x in range(n):
        fetches[2 * x].wait()
        fetches[2 * x + 1].wait()
        for c in range(copies):
            copy = pltpu.make_async_copy(held.at[x], out_ref.at[x, c], stored.at[x, c])
            copy.start()
            stores.append(copy)
    for copy in stores:
        copy.wait()


def packed(left_root, inputs, n, copies):
    share, cols = inputs.shape[0] // n, inputs.shape[1]
    both = left_root.size // (n * copies * cols) + share
    return pl.pallas_call(
        pack,
        in_specs=[
            pl.BlockSpec(memory_space=pltpu.SMEM),
            pl.BlockSpec(memory_space=pl.ANY),
            pl.BlockSpec(memory_space=pl.ANY),
        ],
        out_specs=pl.BlockSpec(memory_space=pl.ANY),
        out_shape=jax.ShapeDtypeStruct((n, copies, both, cols), inputs.dtype),
        scratch_shapes=[
            pltpu.VMEM((n, both, cols), inputs.dtype),
            pltpu.SemaphoreType.DMA((n, 2)),
            pltpu.SemaphoreType.DMA((n, copies)),
        ],
    )(lax.axis_index("y").astype(jnp.int32)[None], left_root, inputs)


def body(out_grad, inputs, left_root, right_root, momentum):
    nx, nz, ny, nk = (lax.axis_size(name) for name in ("x", "z", "y", "core"))
    rows, order = left_root.shape
    cols = inputs.shape[1]
    wide = order // nx
    share = rows // nx
    piece = rows * wide // (ny * cols)

    blocks = packed(left_root, inputs, nx, ny).reshape(nx * ny, piece + share, cols)
    got = lax.all_to_all(blocks, ("x", "y"), 0, 0)
    left = got[:, :piece].reshape(nx, rows // piece, wide // cols, piece, cols)
    left = left.transpose(0, 1, 3, 2, 4).reshape(nx * rows, wide)

    cotangent = lax.all_gather(out_grad.T, "z", axis=0).reshape(wide, -1)

    part = contract(cotangent, left, 0, 1).astype(jnp.bfloat16)
    part = part.reshape(-1, nx, share, nx * rows).transpose(1, 0, 2, 3).reshape(nx, -1, nx * rows)
    part, own = lax.optimization_barrier((part, got[:, piece:].reshape(-1, cols)))
    product = summed_over_x(part).astype(jnp.bfloat16)

    own = lax.all_gather(own, "core", axis=0, tiled=True)
    own = own.reshape(nk, nx * ny, share, cols).transpose(1, 0, 2, 3)
    own = lax.optimization_barrier(own.reshape(nx, ny * nk, share, cols))
    own = own.transpose(0, 2, 1, 3).reshape(rows, -1)
    own = contract(own, right_root, 1, 0).astype(jnp.bfloat16)
    own = jnp.broadcast_to(own, (nz, rows, cols))
    tokens = lax.all_to_all(own, "z", 0, 0)
    tokens = tokens.reshape(nz, nx, share, cols).transpose(1, 0, 2, 3).reshape(-1, cols)
    panel = lax.all_gather(product, COL, axis=0, tiled=True)

    part = contract(panel, tokens, 0, 0).astype(jnp.bfloat16).reshape(nx, rows, cols)
    shaped = summed_over_x(part)
    momentum_new = 0.9 * momentum + shaped
    update = (0.25 * (0.9 * momentum_new + shaped)).astype(jnp.bfloat16)
    return (momentum_new, update)


def solution(mesh):
    split = Mesh(mesh.devices.reshape(4, 16, 8, 2), ("x", "z", "y", "core"))
    in_specs = (P(COL, ROW), P(ROW, COL), P(ROW, None), P(None, COL), P(ROW, COL))
    out_specs = (P(ROW, COL), P(ROW, COL))

    def step(*args):
        return body(*args)

    step = jax.shard_map(step, mesh=split, in_specs=in_specs, out_specs=out_specs, check_vma=False)
    return step
```

time: 111 us -> 115 us (1.036)
  the two profiles are of different devices: /device:TPU:2 before, /device:TPU:8 now
where the time goes in v6:
time: 115 us
  blocking collectives  66.5 us (58%)
  starting transfers between devices  25.1 us (22%)
  waiting for transfers between devices  15.7 us (14%)
  local copies, waits for them, and re-layouts  2.54 us (2%)
  Pallas kernels  2.11 us (2%)
  matrix products  1.16 us (1%)
    all_gather x1, blocking collectives, body(): cotangent = lax.all_gather(out_grad.T, 'z', axis=0).reshape(wide, -1)  38.7 us
    all_gather x1, blocking collectives, body(): panel = lax.all_gather(product, COL, axis=0, tiled=True)  16.9 us
    all_to_all x1, starting transfers between devices, body(): got = lax.all_to_all(blocks, ('x', 'y'), 0, 0)  16.6 us
    all_to_all x1, waiting for transfers between devices, body(): tokens = lax.all_to_all(own, 'z', 0, 0)  10.2 us
    all_to_all x1, blocking collectives, summed_over_x(): parts = lax.all_to_all(parts, 'x', 0, 0)  8.7 us
    all_to_all x1, waiting for transfers between devices, summed_over_x(): parts = lax.all_to_all(parts, 'x', 0, 0)  5.51 us
    all_to_all x1, starting transfers between devices, summed_over_x(): parts = lax.all_to_all(parts, 'x', 0, 0)  4.26 us
    all_to_all x1, starting transfers between devices, body(): tokens = lax.all_to_all(own, 'z', 0, 0)  4.24 us
  transfers between devices with their start and end apart: 3, of which 2 were waited for; matrix products, arithmetic and copies ran while one was open for 0% of the time, Pallas kernels for 0%

profile of v6, /device:TPU:8, one launch (start us, length us, event | category | flops | bytes accessed | tf_op | source)
XLA Modules:
  0.0 114.6 jit_solution(16559563686107637124)
XLA Ops:
  0.6 0.0 copy-start
  0.6 0.0 copy-start.2
  0.7 2.1 %shard_map.68 = bf16[4,8,48,256]{3,2,1,0:T(8,128)(2,1)} custom-call(s32[1]{0:T(128)} %bitcast.place_ref, bf16[64,4096]{1,0:T(8,128)(2,1)} %left_ref.1, bf16[64,256]{1,0:T(8,128)(2,1)} %own_ref.1), custom_call_target="tpu_custom_call" | custom-call | tf_op jit(solution)/shard_map/pallas_call | solution.py:57
  2.8 16.6 %all-to-all-start = ((bf16[32,48,256]{2,1,0:T(8,128)(2,1)}), bf16[32,48,256]{2,1,0:T(8,128)(2,1)S(1)}, u32[]{:S(2)}, u32[]{:S(2)}) async-start(bf16[32,48,256]{2,1,0:T(8,128)(2,1)} %bitcast.45), calls=%async_computation | async-start | bytes 1572864 | tf_op jit(solution)/shard_map/all_to_all | solution.py:83
  19.4 0.0 copy-done.2
  19.4 38.7 %all-gather = bf16[1024,256]{1,0:T(8,128)(2,1)S(1)} all-gather(bf16[64,256]{1,0:T(8,128)(2,1)S(1)} %bitcast.58), channel_id=2, replica_groups=mesh['x'=4,'z'=16,'y'=8,'core'=2] {'z'}, dimensions={0}, use_global_device_ids=true | all-gather | bytes 557056 | tf_op jit(solution)/shard_map/all_gather | solution.py:87
  58.2 0.0 all-to-all-done
  58.2 0.1 slice.40
  58.2 0.4 copy.9
  58.7 0.1 copy.14
  58.8 0.4 convolution_convert_fusion.1
  59.1 0.7 copy.10
  59.8 2.2 %all_gather.15 = bf16[1024,256]{1,0:T(8,128)(2,1)S(1)} all-gather(bf16[512,256]{1,0:T(8,128)(2,1)S(1)} %bitcast.54), channel_id=1, replica_groups=mesh['x'=4,'z'=16,'y'=8,'core'=2] {'core'}, dimensions={0}, use_global_device_ids=true | all-gather | bytes 786432 | tf_op jit(solution)/shard_map/all_gather | solution.py:94
  62.0 0.1 copy.11
  62.0 0.2 copy.12
  62.2 0.2 copy.15
  62.4 4.3 %all-to-all-start.1 = ((bf16[4,64,256]{2,1,0:T(8,128)(2,1)}), bf16[4,64,256]{2,1,0:T(8,128)(2,1)S(1)}, u32[]{:S(2)}, u32[]{:S(2)}) async-start(bf16[4,64,256]{2,1,0:T(8,128)(2,1)} %bitcast.8), calls=%async_computation.1 | async-start | bytes 262144 | tf_op jit(solution)/shard_map/all_to_all | solution.py:19
  66.7 0.0 copy-done
  66.7 0.5 convolution_convert_fusion.2
  67.1 5.5 %all-to-all-done.1 = bf16[4,64,256]{2,1,0:T(8,128)(2,1)S(1)} async-done(((bf16[4,64,256]{2,1,0:T(8,128)(2,1)}), bf16[4,64,256]{2,1,0:T(8,128)(2,1)S(1)}, u32[]{:S(2)}, u32[]{:S(2)}) %all-to-all-start.1) | async-done | bytes 131104 | tf_op jit(solution)/shard_map/all_to_all | solution.py:19
  72.6 0.8 broadcast_in_dim.7
  73.5 0.0 copy-start.1
  73.5 4.2 %all-to-all-start.2 = ((bf16[16,64,256]{2,1,0:T(8,128)(2,1)}), bf16[16,64,256]{2,1,0:T(8,128)(2,1)S(1)}, u32[]{:S(2)}, u32[]{:S(2)}) async-start(bf16[16,64,256]{2,1,0:T(8,128)(2,1)} %broadcast_in_dim.7), calls=%async_computation.2 | async-start | bytes 1048576 | tf_op jit(solution)/shard_map/all_to_all | solution.py:100
  77.8 16.9 %all-gather.1 = bf16[1,1024,256]{2,1,0:T(8,128)(2,1)S(1)} all-gather(bf16[1,64,256]{2,1,0:T(8,128)(2,1)S(1)} %add_convert_fusion), channel_id=3, replica_groups=mesh['x'=4,'z'=16,'y'=8,'core'=2] {'y','core'}, dimensions={1}, use_global_device_ids=true | all-gather | bytes 557056 | tf_op jit(solution)/shard_map/all_gather | solution.py:102
  94.6 10.2 %all-to-all-done.2 = bf16[16,64,256]{2,1,0:T(8,128)(2,1)S(1)} async-done(((bf16[16,64,256]{2,1,0:T(8,128)(2,1)}), bf16[16,64,256]{2,1,0:T(8,128)(2,1)S(1)}, u32[]{:S(2)}, u32[]{:S(2)}) %all-to-all-start.2) | async-done | bytes 524320 | tf_op jit(solution)/shard_map/all_to_all | solution.py:100
  104.9 0.3 convolution_convert_fusion
  105.2 8.7 %all_to_all.20 = bf16[4,64,256]{2,1,0:T(8,128)(2,1)S(1)} all-to-all(bf16[4,64,256]{2,1,0:T(8,128)(2,1)S(1)} %bitcast.57), channel_id=1, replica_groups=mesh['x'=4,'z'=16,'y'=8,'core'=2] {'x'}, dimensions={0} | all-to-all | bytes 262144 | tf_op jit(solution)/shard_map/all_to_all | solution.py:19
  113.9 0.0 copy-done.1
  113.9 0.7 fusion.2
  (3 shorter events, 0.1 us)
Async XLA Ops:
  0.6 66.0 %copy-start = (bf16[4096,256]{1,0:T(8,128)(2,1)S(1)}, bf16[4096,256]{1,0:T(8,128)(2,1)}, u32[]{:S(2)}) copy-start(bf16[4096,256]{1,0:T(8,128)(2,1)} %param.8) | copy-start | bytes 6291460
  0.6 18.8 %copy-start.2 = (bf16[256,64]{0,1:T(8,128)(2,1)S(1)}, bf16[256,64]{0,1:T(8,128)(2,1)}, u32[]{:S(2)}) copy-start(bf16[256,64]{0,1:T(8,128)(2,1)} %param.5) | copy-start | bytes 98308
  2.8 55.4 %all-to-all-start = ((bf16[32,48,256]{2,1,0:T(8,128)(2,1)}), bf16[32,48,256]{2,1,0:T(8,128)(2,1)S(1)}, u32[]{:S(2)}, u32[]{:S(2)}) async-start(bf16[32,48,256]{2,1,0:T(8,128)(2,1)} %bitcast.45), calls=%async_computation | async-start | bytes 1572864 | tf_op jit(solution)/shard_map/all_to_all | solution.py:83
  62.4 10.2 %all-to-all-start.1 = ((bf16[4,64,256]{2,1,0:T(8,128)(2,1)}), bf16[4,64,256]{2,1,0:T(8,128)(2,1)S(1)}, u32[]{:S(2)}, u32[]{:S(2)}) async-start(bf16[4,64,256]{2,1,0:T(8,128)(2,1)} %bitcast.8), calls=%async_computation.1 | async-start | bytes 262144 | tf_op jit(solution)/shard_map/all_to_all | solution.py:19
  73.5 40.4 %copy-start.1 = (f32[64,256]{1,0:T(8,128)S(1)}, f32[64,256]{1,0:T(8,128)}, u32[]{:S(2)}) copy-start(f32[64,256]{1,0:T(8,128)} %param.9) | copy-start | bytes 196612
  73.5 31.3 %all-to-all-start.2 = ((bf16[16,64,256]{2,1,0:T(8,128)(2,1)}), bf16[16,64,256]{2,1,0:T(8,128)(2,1)S(1)}, u32[]{:S(2)}, u32[]{:S(2)}) async-start(bf16[16,64,256]{2,1,0:T(8,128)(2,1)} %broadcast_in_dim.7), calls=%async_computation.2 | async-start | bytes 1048576 | tf_op jit(solution)/shard_map/all_to_all | solution.py:100

commit v7 on v5

--- a/solution.py
+++ b/solution.py
@@ -80,17 +80,18 @@
         got = lax.all_to_all(blocks, ("x", COL), 0, 0)
     left = got[:, :share].reshape(nx, rows // share, wide // cols, share, cols)
     left = left.transpose(0, 1, 3, 2, 4).reshape(nx * rows, wide)
-    own = got[:, share:].reshape(nx, nc, share, cols).transpose(0, 2, 1, 3).reshape(rows, -1)
 
     with jax.named_scope("cotangent"):
-        cotangent = lax.all_gather(out_grad.T, "z", axis=0, tiled=True)
+        cotangent = lax.all_gather(out_grad.T, "z", axis=0).reshape(wide, -1)
 
     part = contract(cotangent, left, 0, 1).astype(jnp.bfloat16)
     part = part.reshape(-1, nx, share, nx * rows).transpose(1, 0, 2, 3).reshape(nx, -1, nx * rows)
+    part, got = lax.optimization_barrier((part, got))
+    own = got[:, share:].reshape(nx, nc, share, cols).transpose(0, 2, 1, 3).reshape(rows, -1)
+    own = contract(own, right_root, 1, 0).astype(jnp.bfloat16)
+    part, own = lax.optimization_barrier((part, jnp.broadcast_to(own, (nz, rows, cols))))
     product = summed_over_x(part).astype(jnp.bfloat16)
 
-    own = contract(own, right_root, 1, 0).astype(jnp.bfloat16)
-    own = jnp.broadcast_to(own, (nz, rows, cols))
     tokens = lax.all_to_all(own, "z", 0, 0)
     tokens = tokens.reshape(nz, nx, share, cols).transpose(1, 0, 2, 3).reshape(-1, cols)
     panel = lax.all_gather(product, COL, axis=0, tiled=True)

time: 111 us -> 111 us (level)
  blocking collectives: 67.6 us -> 76.7 us
  starting transfers between devices: 26.2 us -> 21.3 us
  waiting for transfers between devices: 8.64 us -> 4.73 us
    all_to_all x1 -> x2, blocking collectives: 8.37 us -> 17.6 us  [summed_over_x(): parts = lax.all_to_all(parts, 'x', 0, 0)]
    all_to_all x1 -> x0, starting transfers between devices: 4.89 us -> none  [summed_over_x(): parts = lax.all_to_all(parts, 'x', 0, 0)]
    all_to_all x1 -> x0, waiting for transfers between devices: 3.68 us -> none  [summed_over_x(): parts = lax.all_to_all(parts, 'x', 0, 0)]
  transfers between devices with their start and end apart: 3 -> 2, of which waited for: 2 -> 1; matrix products, arithmetic and copies ran while one was open for 1% -> 0% of each run, Pallas kernels for 0% -> 0%
where the time goes in v7:
time: 111 us; the launch traced here: 110 us
  blocking collectives  76.7 us (69%)
  starting transfers between devices  21.3 us (19%)
  waiting for transfers between devices  4.73 us (4%)
  Pallas kernels  2.48 us (2%)
  local copies, waits for them, and re-layouts  2.32 us (2%)
  matrix products  1.16 us (1%)
    all_gather x1, blocking collectives, body(): cotangent = lax.all_gather(out_grad.T, 'z', axis=0).reshape(wide, -1)  40.9 us
    all_gather x1, blocking collectives, body(): panel = lax.all_gather(product, COL, axis=0, tiled=True)  18.3 us
    all_to_all x2, blocking collectives, summed_over_x(): parts = lax.all_to_all(parts, 'x', 0, 0)  17.6 us
    all_to_all x1, starting transfers between devices, body(): got = lax.all_to_all(blocks, ('x', COL), 0, 0)  17.4 us
    all_to_all x1, waiting for transfers between devices, body(): tokens = lax.all_to_all(own, 'z', 0, 0)  4.73 us
    all_to_all x1, starting transfers between devices, body(): tokens = lax.all_to_all(own, 'z', 0, 0)  3.99 us
    pallas_call x1, Pallas kernels, packed(): pl.pallas_call(pack, in_specs=[pl.BlockSpec(memory_space=pltpu.SMEM), pl....  2.48 us
  transfers between devices with their start and end apart: 2, of which 1 were waited for; matrix products, arithmetic and copies ran while one was open for 0% of the time, Pallas kernels for 0%

profile of v7, /device:TPU:2, one launch (start us, length us, event | category | flops | bytes accessed | tf_op | source)
XLA Modules:
  0.0 110.2 jit_solution(1974147137370522381)
XLA Ops:
  0.6 0.0 copy-start
  0.6 0.0 copy-start.3
  0.7 2.5 %shard_map.68 = bf16[4,16,32,256]{3,2,1,0:T(8,128)(2,1)} custom-call(s32[1]{0:T(128)} %bitcast.place_ref, bf16[64,4096]{1,0:T(8,128)(2,1)} %left_ref.1, bf16[64,256]{1,0:T(8,128)(2,1)} %own_ref.1), custom_call_target="tpu_custom_call" | custom-call | tf_op jit(solution)/shard_map/pallas_call | solution.py:54
  3.1 17.4 %all-to-all-start = ((bf16[64,32,256]{2,1,0:T(8,128)(2,1)}), bf16[64,32,256]{2,1,0:T(8,128)(2,1)S(1)}, u32[]{:S(2)}, u32[]{:S(2)}) async-start(bf16[64,32,256]{2,1,0:T(8,128)(2,1)} %bitcast.42), calls=%async_computation | async-start | bytes 2097152 | tf_op jit(solution)/shard_map/turn/all_to_all | solution.py:80
  20.5 0.0 copy-done.3
  20.5 40.9 %all-gather = bf16[1024,256]{1,0:T(8,128)(2,1)} all-gather(bf16[64,256]{1,0:T(8,128)(2,1)S(1)} %bitcast.54), channel_id=2, replica_groups=mesh['x'=4,'z'=16,'col'=16] {'z'}, dimensions={0}, use_global_device_ids=true | all-gather | bytes 557056 | tf_op jit(solution)/shard_map/cotangent/all_gather | solution.py:85
  61.4 0.0 all-to-all-done
  61.4 0.0 copy-start.1
  61.4 0.3 copy.8
  61.7 0.1 copy.12
  61.8 0.6 copy-done.1
  62.4 0.3 convolution_convert_fusion.1
  62.8 0.2 copy.10
  63.0 0.2 copy.13
  63.2 0.0 copy-done
  63.2 0.5 convolution_convert_fusion.2
  63.7 0.9 broadcast_in_dim.7
  64.5 9.2 %all_to_all.20 = bf16[4,64,256]{2,1,0:T(8,128)(2,1)S(1)} all-to-all(bf16[4,64,256]{2,1,0:T(8,128)(2,1)S(1)} %bitcast.52), channel_id=1, replica_groups=mesh['x'=4,'z'=16,'col'=16] {'x'}, dimensions={0} | all-to-all | bytes 262144 | tf_op jit(solution)/shard_map/all_to_all | solution.py:18
  73.7 0.0 copy-start.2
  73.7 4.0 %all-to-all-start.2 = ((bf16[16,64,256]{2,1,0:T(8,128)(2,1)}), bf16[16,64,256]{2,1,0:T(8,128)(2,1)S(1)}, u32[]{:S(2)}, u32[]{:S(2)}) async-start(bf16[16,64,256]{2,1,0:T(8,128)(2,1)} %broadcast_in_dim.7), calls=%async_computation.2 | async-start | bytes 1048576 | tf_op jit(solution)/shard_map/all_to_all | solution.py:95
  77.8 18.3 %all-gather.1 = bf16[1,1024,256]{2,1,0:T(8,128)(2,1)S(1)} all-gather(bf16[1,64,256]{2,1,0:T(8,128)(2,1)S(1)} %add_convert_fusion), channel_id=3, replica_groups=mesh['x'=4,'z'=16,'col'=16] {'col'}, dimensions={1}, use_global_device_ids=true | all-gather | bytes 557056 | tf_op jit(solution)/shard_map/all_gather | solution.py:97
  96.1 4.7 %all-to-all-done.2 = bf16[16,64,256]{2,1,0:T(8,128)(2,1)S(1)} async-done(((bf16[16,64,256]{2,1,0:T(8,128)(2,1)}), bf16[16,64,256]{2,1,0:T(8,128)(2,1)S(1)}, u32[]{:S(2)}, u32[]{:S(2)}) %all-to-all-start.2) | async-done | bytes 524320 | tf_op jit(solution)/shard_map/all_to_all | solution.py:95
  100.8 0.3 convolution_convert_fusion
  101.2 8.4 %all_to_all.21 = bf16[4,64,256]{2,1,0:T(8,128)(2,1)S(1)} all-to-all(bf16[4,64,256]{2,1,0:T(8,128)(2,1)S(1)} %bitcast.53), channel_id=1, replica_groups=mesh['x'=4,'z'=16,'col'=16] {'x'}, dimensions={0} | all-to-all | bytes 262144 | tf_op jit(solution)/shard_map/all_to_all | solution.py:18
  109.6 0.0 copy-done.2
  109.6 0.7 fusion.2
  (5 shorter events, 0.1 us)
Async XLA Ops:
  0.6 62.6 %copy-start = (bf16[4096,256]{1,0:T(8,128)(2,1)S(1)}, bf16[4096,256]{1,0:T(8,128)(2,1)}, u32[]{:S(2)}) copy-start(bf16[4096,256]{1,0:T(8,128)(2,1)} %param.8) | copy-start | bytes 6291460
  0.6 19.9 %copy-start.3 = (bf16[256,64]{0,1:T(8,128)(2,1)S(1)}, bf16[256,64]{0,1:T(8,128)(2,1)}, u32[]{:S(2)}) copy-start(bf16[256,64]{0,1:T(8,128)(2,1)} %param.5) | copy-start | bytes 98308
  3.1 58.2 %all-to-all-start = ((bf16[64,32,256]{2,1,0:T(8,128)(2,1)}), bf16[64,32,256]{2,1,0:T(8,128)(2,1)S(1)}, u32[]{:S(2)}, u32[]{:S(2)}) async-start(bf16[64,32,256]{2,1,0:T(8,128)(2,1)} %bitcast.42), calls=%async_computation | async-start | bytes 2097152 | tf_op jit(solution)/shard_map/turn/all_to_all | solution.py:80
  61.4 1.0 copy-start.1
  73.7 35.8 %copy-start.2 = (f32[64,256]{1,0:T(8,128)S(1)}, f32[64,256]{1,0:T(8,128)}, u32[]{:S(2)}) copy-start(f32[64,256]{1,0:T(8,128)} %param.9) | copy-start | bytes 196612
  73.7 27.1 %all-to-all-start.2 = ((bf16[16,64,256]{2,1,0:T(8,128)(2,1)}), bf16[16,64,256]{2,1,0:T(8,128)(2,1)S(1)}, u32[]{:S(2)}, u32[]{:S(2)}) async-start(bf16[16,64,256]{2,1,0:T(8,128)(2,1)} %broadcast_in_dim.7), calls=%async_computation.2 | async-start | bytes 1048576 | tf_op jit(solution)/shard_map/all_to_all | solution.py:95

commit v8 on v7

--- a/solution.py
+++ b/solution.py
@@ -68,6 +68,39 @@
     )(lax.axis_index(COL).astype(jnp.int32)[None], left_root, inputs)
 
 
+def spread(got_ref, right_ref, out_ref, own, right, fetched):
+    n, copies, share, cols = own.shape
+    copy_own = pltpu.make_async_copy(got_ref.at[:, :, pl.ds(share, share)], own, fetched.at[copies])
+    copy_own.start()
+    fetches = []
+    for c in range(copies):
+        copy = pltpu.make_async_copy(right_ref.at[pl.ds(c * cols, cols)], right.at[c], fetched.at[c])
+        copy.start()
+        fetches.append(copy)
+    copy_own.wait()
+    total = jnp.zeros((n * share, cols), jnp.float32)
+    for c in range(copies):
+        fetches[c].wait()
+        total += jnp.dot(own[:, c].reshape(n * share, cols), right[c], preferred_element_type=jnp.float32)
+    out_ref[...] = jnp.broadcast_to(total.astype(out_ref.dtype), out_ref.shape)
+
+
+def spread_product(got, right_root, copies):
+    n, nc, both, cols = got.shape
+    share = both // 2
+    return pl.pallas_call(
+        spread,
+        in_specs=[pl.BlockSpec(memory_space=pl.ANY)] * 2,
+        out_specs=pl.BlockSpec(memory_space=pltpu.VMEM),
+        out_shape=jax.ShapeDtypeStruct((copies, n * share, cols), got.dtype),
+        scratch_shapes=[
+            pltpu.VMEM((n, nc, share, cols), got.dtype),
+            pltpu.VMEM((nc, cols, cols), got.dtype),
+            pltpu.SemaphoreType.DMA((nc + 1,)),
+        ],
+    )(got, right_root)
+
+
 def body(out_grad, inputs, left_root, right_root, momentum):
     nx, nz, nc = lax.axis_size("x"), lax.axis_size("z"), lax.axis_size(COL)
     rows, order = left_root.shape
@@ -87,9 +120,8 @@
     part = contract(cotangent, left, 0, 1).astype(jnp.bfloat16)
     part = part.reshape(-1, nx, share, nx * rows).transpose(1, 0, 2, 3).reshape(nx, -1, nx * rows)
     part, got = lax.optimization_barrier((part, got))
-    own = got[:, share:].reshape(nx, nc, share, cols).transpose(0, 2, 1, 3).reshape(rows, -1)
-    own = contract(own, right_root, 1, 0).astype(jnp.bfloat16)
-    part, own = lax.optimization_barrier((part, jnp.broadcast_to(own, (nz, rows, cols))))
+    own = spread_product(got.reshape(nx, nc, 2 * share, cols), right_root, nz)
+    part, own = lax.optimization_barrier((part, own))
     product = summed_over_x(part).astype(jnp.bfloat16)
 
     tokens = lax.all_to_all(own, "z", 0, 0)

time: 111 us -> 112 us (level)
  the two profiles are of different devices: /device:TPU:2 before, /device:TPU:8 now
where the time goes in v8:
time: 112 us; the launch traced here: 111 us
  blocking collectives  74.2 us (66%)
  starting transfers between devices  21.4 us (19%)
  waiting for transfers between devices  7.66 us (7%)
  Pallas kernels  5.47 us (5%)
    all_gather x1, blocking collectives, body(): cotangent = lax.all_gather(out_grad.T, 'z', axis=0).reshape(wide, -1)  38.6 us
    all_to_all x2, blocking collectives, summed_over_x(): parts = lax.all_to_all(parts, 'x', 0, 0)  18.5 us
    all_to_all x1, starting transfers between devices, body(): got = lax.all_to_all(blocks, ('x', COL), 0, 0)  17.2 us
    all_gather x1, blocking collectives, body(): panel = lax.all_gather(product, COL, axis=0, tiled=True)  17.1 us
    all_to_all x1, waiting for transfers between devices, body(): tokens = lax.all_to_all(own, 'z', 0, 0)  7.66 us
    all_to_all x1, starting transfers between devices, body(): tokens = lax.all_to_all(own, 'z', 0, 0)  4.19 us
    pallas_call x1, Pallas kernels, spread_product(): pl.pallas_call(spread, in_specs=[pl.BlockSpec(memory_space=pl.ANY)] * 2,...  3.14 us
    pallas_call x1, Pallas kernels, packed(): pl.pallas_call(pack, in_specs=[pl.BlockSpec(memory_space=pltpu.SMEM), pl....  2.34 us
  transfers between devices with their start and end apart: 2, of which 1 were waited for; matrix products, arithmetic and copies ran while one was open for 0% of the time, Pallas kernels for 0%

profile of v8, /device:TPU:8, one launch (start us, length us, event | category | flops | bytes accessed | tf_op | source)
XLA Modules:
  0.0 111.5 jit_solution(126909947564236984)
XLA Ops:
  0.6 0.0 copy-start.2
  0.6 2.3 %shard_map.68 = bf16[4,16,32,256]{3,2,1,0:T(8,128)(2,1)} custom-call(s32[1]{0:T(128)} %bitcast.place_ref, bf16[64,4096]{1,0:T(8,128)(2,1)} %left_ref.1, bf16[64,256]{1,0:T(8,128)(2,1)} %own_ref.1), custom_call_target="tpu_custom_call" | custom-call | tf_op jit(solution)/shard_map/pallas_call | solution.py:54
  3.0 17.2 %all-to-all-start = ((bf16[64,32,256]{2,1,0:T(8,128)(2,1)}), bf16[64,32,256]{2,1,0:T(8,128)(2,1)S(1)}, u32[]{:S(2)}, u32[]{:S(2)}) async-start(bf16[64,32,256]{2,1,0:T(8,128)(2,1)} %bitcast.36), calls=%async_computation | async-start | bytes 2097152 | tf_op jit(solution)/shard_map/turn/all_to_all | solution.py:113
  20.2 0.0 copy-done.2
  20.2 38.6 %all-gather = bf16[1024,256]{1,0:T(8,128)(2,1)S(1)} all-gather(bf16[64,256]{1,0:T(8,128)(2,1)S(1)} %bitcast.45), channel_id=2, replica_groups=mesh['x'=4,'z'=16,'col'=16] {'z'}, dimensions={0}, use_global_device_ids=true | all-gather | bytes 557056 | tf_op jit(solution)/shard_map/cotangent/all_gather | solution.py:118
  58.8 0.0 all-to-all-done
  58.8 0.0 copy-start
  58.9 0.3 copy.9
  59.1 0.1 copy.12
  59.2 0.4 convolution_convert_fusion.1
  59.6 0.2 copy-done
  59.8 3.1 %shard_map.69 = bf16[16,64,256]{2,1,0:T(8,128)(2,1)} custom-call(bf16[4,16,32,256]{3,2,1,0:T(8,128)(2,1)} %bitcast.35, bf16[4096,256]{1,0:T(8,128)(2,1)} %right_ref.1), custom_call_target="tpu_custom_call" | custom-call | tf_op jit(solution)/shard_map/pallas_call | solution.py:91
  62.9 10.1 %all_to_all.20 = bf16[4,64,256]{2,1,0:T(8,128)(2,1)S(1)} all-to-all(bf16[4,64,256]{2,1,0:T(8,128)(2,1)S(1)} %bitcast.43), channel_id=1, replica_groups=mesh['x'=4,'z'=16,'col'=16] {'x'}, dimensions={0} | all-to-all | bytes 262144 | tf_op jit(solution)/shard_map/all_to_all | solution.py:18
  73.1 0.0 copy-start.1
  73.1 4.2 %all-to-all-start.2 = ((bf16[16,64,256]{2,1,0:T(8,128)(2,1)}), bf16[16,64,256]{2,1,0:T(8,128)(2,1)S(1)}, u32[]{:S(2)}, u32[]{:S(2)}) async-start(bf16[16,64,256]{2,1,0:T(8,128)(2,1)} %shard_map.69), calls=%async_computation.2 | async-start | bytes 1048576 | tf_op jit(solution)/shard_map/all_to_all | solution.py:127
  77.3 17.1 %all-gather.1 = bf16[1,1024,256]{2,1,0:T(8,128)(2,1)S(1)} all-gather(bf16[1,64,256]{2,1,0:T(8,128)(2,1)S(1)} %add_convert_fusion), channel_id=3, replica_groups=mesh['x'=4,'z'=16,'col'=16] {'col'}, dimensions={1}, use_global_device_ids=true | all-gather | bytes 557056 | tf_op jit(solution)/shard_map/all_gather | solution.py:129
  94.4 7.7 %all-to-all-done.2 = bf16[16,64,256]{2,1,0:T(8,128)(2,1)S(1)} async-done(((bf16[16,64,256]{2,1,0:T(8,128)(2,1)}), bf16[16,64,256]{2,1,0:T(8,128)(2,1)S(1)}, u32[]{:S(2)}, u32[]{:S(2)}) %all-to-all-start.2) | async-done | bytes 524320 | tf_op jit(solution)/shard_map/all_to_all | solution.py:127
  102.1 0.3 convolution_convert_fusion
  102.4 8.4 %all_to_all.21 = bf16[4,64,256]{2,1,0:T(8,128)(2,1)S(1)} all-to-all(bf16[4,64,256]{2,1,0:T(8,128)(2,1)S(1)} %bitcast.44), channel_id=1, replica_groups=mesh['x'=4,'z'=16,'col'=16] {'x'}, dimensions={0} | all-to-all | bytes 262144 | tf_op jit(solution)/shard_map/all_to_all | solution.py:18
  110.8 0.0 copy-done.1
  110.8 0.7 fusion.2
  (4 shorter events, 0.1 us)
Async XLA Ops:
  0.6 19.5 %copy-start.2 = (bf16[256,64]{0,1:T(8,128)(2,1)S(1)}, bf16[256,64]{0,1:T(8,128)(2,1)}, u32[]{:S(2)}) copy-start(bf16[256,64]{0,1:T(8,128)(2,1)} %param.5) | copy-start | bytes 98308
  3.0 55.8 %all-to-all-start = ((bf16[64,32,256]{2,1,0:T(8,128)(2,1)}), bf16[64,32,256]{2,1,0:T(8,128)(2,1)S(1)}, u32[]{:S(2)}, u32[]{:S(2)}) async-start(bf16[64,32,256]{2,1,0:T(8,128)(2,1)} %bitcast.36), calls=%async_computation | async-start | bytes 2097152 | tf_op jit(solution)/shard_map/turn/all_to_all | solution.py:113
  58.8 1.0 copy-start
  73.1 37.7 %copy-start.1 = (f32[64,256]{1,0:T(8,128)S(1)}, f32[64,256]{1,0:T(8,128)}, u32[]{:S(2)}) copy-start(f32[64,256]{1,0:T(8,128)} %param.9) | copy-start | bytes 196612
  73.1 29.0 %all-to-all-start.2 = ((bf16[16,64,256]{2,1,0:T(8,128)(2,1)}), bf16[16,64,256]{2,1,0:T(8,128)(2,1)S(1)}, u32[]{:S(2)}, u32[]{:S(2)}) async-start(bf16[16,64,256]{2,1,0:T(8,128)(2,1)} %shard_map.69), calls=%async_computation.2 | async-start | bytes 1048576 | tf_op jit(solution)/shard_map/all_to_all | solution.py:127

commit v9 on v8

--- a/solution.py
+++ b/solution.py
@@ -5,6 +5,7 @@
 from jax.experimental.pallas import tpu as pltpu
 from jax.sharding import Mesh
 from jax.sharding import PartitionSpec as P
+
 
 ROW = ("x", "z")
 COL = "col"
@@ -109,20 +110,17 @@
     share = rows // nx
 
     blocks = packed(left_root, inputs, nx, nc).reshape(nx * nc, 2 * share, cols)
-    with jax.named_scope("turn"):
-        got = lax.all_to_all(blocks, ("x", COL), 0, 0)
+    got = lax.all_to_all(blocks, ("x", COL), 0, 0)
     left = got[:, :share].reshape(nx, rows // share, wide // cols, share, cols)
     left = left.transpose(0, 1, 3, 2, 4).reshape(nx * rows, wide)
 
-    with jax.named_scope("cotangent"):
-        cotangent = lax.all_gather(out_grad.T, "z", axis=0).reshape(wide, -1)
+    cotangent = lax.all_gather(out_grad.T, "z", axis=0).reshape(wide, -1)
 
     part = contract(cotangent, left, 0, 1).astype(jnp.bfloat16)
     part = part.reshape(-1, nx, share, nx * rows).transpose(1, 0, 2, 3).reshape(nx, -1, nx * rows)
     part, got = lax.optimization_barrier((part, got))
+    product = summed_over_x(part).astype(jnp.bfloat16)
     own = spread_product(got.reshape(nx, nc, 2 * share, cols), right_root, nz)
-    part, own = lax.optimization_barrier((part, own))
-    product = summed_over_x(part).astype(jnp.bfloat16)
 
     tokens = lax.all_to_all(own, "z", 0, 0)
     tokens = tokens.reshape(nz, nx, share, cols).transpose(1, 0, 2, 3).reshape(-1, cols)
@@ -139,4 +137,9 @@
     split = Mesh(mesh.devices.reshape(4, 16, mesh.shape["col"]), ("x", "z", "col"))
     in_specs = (P("col", ROW), P(ROW, "col"), P(ROW, None), P(None, "col"), P(ROW, "col"))
     out_specs = (P(ROW, "col"), P(ROW, "col"))
-    return jax.shard_map(body, mesh=split, in_specs=in_specs, out_specs=out_specs, check_vma=False)
+
+    def step(*args):
+        return body(*args)
+
+    step = jax.shard_map(step, mesh=split, in_specs=in_specs, out_specs=out_specs, check_vma=False)
+    return step

time: 112 us -> 110 us (0.982)
  blocking collectives: 74.2 us -> 64.5 us
  starting transfers between devices: 21.4 us -> 25.6 us
  waiting for transfers between devices: 7.66 us -> 10.5 us
    all_to_all x2 -> x1, blocking collectives: 18.5 us -> 8.73 us  [summed_over_x(): parts = lax.all_to_all(parts, 'x', 0, 0)]
    all_to_all x0 -> x1, starting transfers between devices: none -> 4.36 us  [summed_over_x(): parts = lax.all_to_all(parts, 'x', 0, 0)]
    all_to_all x0 -> x1, waiting for transfers between devices: none -> 2.81 us  [summed_over_x(): parts = lax.all_to_all(parts, 'x', 0, 0)]
  transfers between devices with their start and end apart: 2 -> 3, of which waited for: 1 -> 2; matrix products, arithmetic and copies ran while one was open for 0% -> 0% of each run, Pallas kernels for 0% -> 3%
where the time goes in v9:
time: 110 us; the launch traced here: 109 us
  blocking collectives  64.5 us (59%)
  starting transfers between devices  25.6 us (23%)
  waiting for transfers between devices  10.5 us (10%)
  Pallas kernels  5.47 us (5%)
  local copies, waits for them, and re-layouts  1.3 us (1%)
    all_gather x1, blocking collectives, body(): cotangent = lax.all_gather(out_grad.T, 'z', axis=0).reshape(wide, -1)  38.6 us
    all_to_all x1, starting transfers between devices, body(): got = lax.all_to_all(blocks, ('x', COL), 0, 0)  17.2 us
    all_gather x1, blocking collectives, body(): panel = lax.all_gather(product, COL, axis=0, tiled=True)  17.1 us
    all_to_all x1, blocking collectives, summed_over_x(): parts = lax.all_to_all(parts, 'x', 0, 0)  8.73 us
    all_to_all x1, waiting for transfers between devices, body(): tokens = lax.all_to_all(own, 'z', 0, 0)  7.67 us
    all_to_all x1, starting transfers between devices, summed_over_x(): parts = lax.all_to_all(parts, 'x', 0, 0)  4.36 us
    all_to_all x1, starting transfers between devices, body(): tokens = lax.all_to_all(own, 'z', 0, 0)  4.05 us
    pallas_call x1, Pallas kernels, spread_product(): pl.pallas_call(spread, in_specs=[pl.BlockSpec(memory_space=pl.ANY)] * 2,...  3.15 us
  transfers between devices with their start and end apart: 3, of which 2 were waited for; matrix products, arithmetic and copies ran while one was open for 0% of the time, Pallas kernels for 3%

profile of v9, /device:TPU:8, one launch (start us, length us, event | category | flops | bytes accessed | tf_op | source)
XLA Modules:
  0.0 109.4 jit_solution(10402540496466392806)
XLA Ops:
  0.6 0.0 copy-start.2
  0.6 2.3 %shard_map.68 = bf16[4,16,32,256]{3,2,1,0:T(8,128)(2,1)} custom-call(s32[1]{0:T(128)} %bitcast.place_ref, bf16[64,4096]{1,0:T(8,128)(2,1)} %left_ref.1, bf16[64,256]{1,0:T(8,128)(2,1)} %own_ref.1), custom_call_target="tpu_custom_call" | custom-call | tf_op jit(solution)/shard_map/pallas_call | solution.py:55
  3.0 17.2 %all-to-all-start = ((bf16[64,32,256]{2,1,0:T(8,128)(2,1)}), bf16[64,32,256]{2,1,0:T(8,128)(2,1)S(1)}, u32[]{:S(2)}, u32[]{:S(2)}) async-start(bf16[64,32,256]{2,1,0:T(8,128)(2,1)} %bitcast.36), calls=%async_computation | async-start | bytes 2097152 | tf_op jit(solution)/shard_map/all_to_all | solution.py:113
  20.2 0.0 copy-done.2
  20.2 38.6 %all-gather = bf16[1024,256]{1,0:T(8,128)(2,1)S(1)} all-gather(bf16[64,256]{1,0:T(8,128)(2,1)S(1)} %bitcast.44), channel_id=2, replica_groups=mesh['x'=4,'z'=16,'col'=16] {'z'}, dimensions={0}, use_global_device_ids=true | all-gather | bytes 557056 | tf_op jit(solution)/shard_map/all_gather | solution.py:117
  58.8 0.0 all-to-all-done
  58.8 0.0 copy-start
  58.9 0.3 copy.9
  59.1 0.1 copy.12
  59.2 0.4 convolution_convert_fusion.1
  59.6 0.2 copy-done
  59.8 0.7 copy.10
  60.4 4.4 %all-to-all-start.1 = ((bf16[4,64,256]{2,1,0:T(8,128)(2,1)}), bf16[4,64,256]{2,1,0:T(8,128)(2,1)S(1)}, u32[]{:S(2)}, u32[]{:S(2)}) async-start(bf16[4,64,256]{2,1,0:T(8,128)(2,1)} %bitcast.8), calls=%async_computation.1 | async-start | bytes 262144 | tf_op jit(solution)/shard_map/all_to_all | solution.py:19
  64.8 3.1 %shard_map.69 = bf16[16,64,256]{2,1,0:T(8,128)(2,1)} custom-call(bf16[4,16,32,256]{3,2,1,0:T(8,128)(2,1)} %bitcast.35, bf16[4096,256]{1,0:T(8,128)(2,1)} %right_ref.1), custom_call_target="tpu_custom_call" | custom-call | tf_op jit(solution)/shard_map/pallas_call | solution.py:92
  67.9 0.0 copy-start.1
  68.0 2.8 %all-to-all-done.1 = bf16[4,64,256]{2,1,0:T(8,128)(2,1)S(1)} async-done(((bf16[4,64,256]{2,1,0:T(8,128)(2,1)}), bf16[4,64,256]{2,1,0:T(8,128)(2,1)S(1)}, u32[]{:S(2)}, u32[]{:S(2)}) %all-to-all-start.1) | async-done | bytes 131104 | tf_op jit(solution)/shard_map/all_to_all | solution.py:19
  70.8 4.1 %all-to-all-start.2 = ((bf16[16,64,256]{2,1,0:T(8,128)(2,1)}), bf16[16,64,256]{2,1,0:T(8,128)(2,1)S(1)}, u32[]{:S(2)}, u32[]{:S(2)}) async-start(bf16[16,64,256]{2,1,0:T(8,128)(2,1)} %shard_map.69), calls=%async_computation.2 | async-start | bytes 1048576 | tf_op jit(solution)/shard_map/all_to_all | solution.py:125
  74.9 17.1 %all-gather.1 = bf16[1,1024,256]{2,1,0:T(8,128)(2,1)S(1)} all-gather(bf16[1,64,256]{2,1,0:T(8,128)(2,1)S(1)} %add_convert_fusion), channel_id=3, replica_groups=mesh['x'=4,'z'=16,'col'=16] {'col'}, dimensions={1}, use_global_device_ids=true | all-gather | bytes 557056 | tf_op jit(solution)/shard_map/all_gather | solution.py:127
  92.0 7.7 %all-to-all-done.2 = bf16[16,64,256]{2,1,0:T(8,128)(2,1)S(1)} async-done(((bf16[16,64,256]{2,1,0:T(8,128)(2,1)}), bf16[16,64,256]{2,1,0:T(8,128)(2,1)S(1)}, u32[]{:S(2)}, u32[]{:S(2)}) %all-to-all-start.2) | async-done | bytes 524320 | tf_op jit(solution)/shard_map/all_to_all | solution.py:125
  99.7 0.3 convolution_convert_fusion
  100.0 8.7 %all_to_all.20 = bf16[4,64,256]{2,1,0:T(8,128)(2,1)S(1)} all-to-all(bf16[4,64,256]{2,1,0:T(8,128)(2,1)S(1)} %bitcast.43), channel_id=1, replica_groups=mesh['x'=4,'z'=16,'col'=16] {'x'}, dimensions={0} | all-to-all | bytes 262144 | tf_op jit(solution)/shard_map/all_to_all | solution.py:19
  108.7 0.0 copy-done.1
  108.7 0.7 fusion.2
  (3 shorter events, 0.1 us)
Async XLA Ops:
  0.6 19.5 %copy-start.2 = (bf16[256,64]{0,1:T(8,128)(2,1)S(1)}, bf16[256,64]{0,1:T(8,128)(2,1)}, u32[]{:S(2)}) copy-start(bf16[256,64]{0,1:T(8,128)(2,1)} %param.5) | copy-start | bytes 98308
  3.0 55.8 %all-to-all-start = ((bf16[64,32,256]{2,1,0:T(8,128)(2,1)}), bf16[64,32,256]{2,1,0:T(8,128)(2,1)S(1)}, u32[]{:S(2)}, u32[]{:S(2)}) async-start(bf16[64,32,256]{2,1,0:T(8,128)(2,1)} %bitcast.36), calls=%async_computation | async-start | bytes 2097152 | tf_op jit(solution)/shard_map/all_to_all | solution.py:113
  58.8 1.0 copy-start
  60.4 10.3 %all-to-all-start.1 = ((bf16[4,64,256]{2,1,0:T(8,128)(2,1)}), bf16[4,64,256]{2,1,0:T(8,128)(2,1)S(1)}, u32[]{:S(2)}, u32[]{:S(2)}) async-start(bf16[4,64,256]{2,1,0:T(8,128)(2,1)} %bitcast.8), calls=%async_computation.1 | async-start | bytes 262144 | tf_op jit(solution)/shard_map/all_to_all | solution.py:19
  67.9 40.8 %copy-start.1 = (f32[64,256]{1,0:T(8,128)S(1)}, f32[64,256]{1,0:T(8,128)}, u32[]{:S(2)}) copy-start(f32[64,256]{1,0:T(8,128)} %param.9) | copy-start | bytes 196612
  70.8 28.8 %all-to-all-start.2 = ((bf16[16,64,256]{2,1,0:T(8,128)(2,1)}), bf16[16,64,256]{2,1,0:T(8,128)(2,1)S(1)}, u32[]{:S(2)}, u32[]{:S(2)}) async-start(bf16[16,64,256]{2,1,0:T(8,128)(2,1)} %shard_map.69), calls=%async_computation.2 | async-start | bytes 1048576 | tf_op jit(solution)/shard_map/all_to_all | solution.py:125

commit v10 on v9

--- a/solution.py
+++ b/solution.py
@@ -99,6 +99,7 @@
             pltpu.VMEM((nc, cols, cols), got.dtype),
             pltpu.SemaphoreType.DMA((nc + 1,)),
         ],
+        compiler_params=pltpu.CompilerParams(vmem_limit_bytes=16 << 20),
     )(got, right_root)
 
 
@@ -119,11 +120,14 @@
     part = contract(cotangent, left, 0, 1).astype(jnp.bfloat16)
     part = part.reshape(-1, nx, share, nx * rows).transpose(1, 0, 2, 3).reshape(nx, -1, nx * rows)
     part, got = lax.optimization_barrier((part, got))
-    product = summed_over_x(part).astype(jnp.bfloat16)
     own = spread_product(got.reshape(nx, nc, 2 * share, cols), right_root, nz)
-
     tokens = lax.all_to_all(own, "z", 0, 0)
     tokens = tokens.reshape(nz, nx, share, cols).transpose(1, 0, 2, 3).reshape(-1, cols)
+
+    parts = lax.all_gather(part.reshape(-1, nx * rows), "x", axis=0, tiled=True).reshape(nx, nx, -1, nx * rows)
+    parts = lax.dynamic_index_in_dim(parts, lax.axis_index("x"), 1, False).astype(jnp.float32)
+    product = (parts[0] + parts[1] if nx == 2 else parts[0] + parts[1] + parts[2] + parts[3]).astype(jnp.bfloat16)
+
     panel = lax.all_gather(product, COL, axis=0, tiled=True)
 
     part = contract(panel, tokens, 0, 0).astype(jnp.bfloat16).reshape(nx, rows, cols)

time: 110 us -> 114 us (1.036)
  the two profiles are of different devices: /device:TPU:8 before, /device:TPU:1 now
where the time goes in v10:
time: 114 us
  blocking collectives  79.4 us (70%)
  starting transfers between devices  23.6 us (21%)
  Pallas kernels  6.33 us (6%)
  local copies, waits for them, and re-layouts  2.19 us (2%)
    all_gather x1, blocking collectives, body(): cotangent = lax.all_gather(out_grad.T, 'z', axis=0).reshape(wide, -1)  34.8 us
    all_gather x1, blocking collectives, body(): panel = lax.all_gather(product, COL, axis=0, tiled=True)  25.8 us
    all_to_all x1, starting transfers between devices, body(): got = lax.all_to_all(blocks, ('x', COL), 0, 0)  18.2 us
    all_gather x1, blocking collectives, body(): lax.all_gather(part.reshape(-1, nx * rows), 'x', axis=0, tiled=True)  10.7 us
    all_to_all x1, blocking collectives, summed_over_x(): parts = lax.all_to_all(parts, 'x', 0, 0)  8.11 us
    all_to_all x1, starting transfers between devices, body(): tokens = lax.all_to_all(own, 'z', 0, 0)  5.39 us
    pallas_call x1, Pallas kernels, spread_product(): pl.pallas_call(spread, in_specs=[pl.BlockSpec(memory_space=pl.ANY)] * 2,...  4 us
    pallas_call x1, Pallas kernels, packed(): pl.pallas_call(pack, in_specs=[pl.BlockSpec(memory_space=pltpu.SMEM), pl....  2.33 us
  transfers between devices with their start and end apart: 2, of which 0 were waited for; matrix products, arithmetic and copies ran while one was open for 0% of the time, Pallas kernels for 0%

profile of v10, /device:TPU:1, one launch (start us, length us, event | category | flops | bytes accessed | tf_op | source)
XLA Modules:
  0.0 113.7 jit_solution(7688769840467824294)
XLA Ops:
  0.6 0.0 copy-start.4
  0.6 2.3 %shard_map.68 = bf16[4,16,32,256]{3,2,1,0:T(8,128)(2,1)} custom-call(s32[1]{0:T(128)} %bitcast.place_ref, bf16[64,4096]{1,0:T(8,128)(2,1)} %left_ref.1, bf16[64,256]{1,0:T(8,128)(2,1)} %own_ref.1), custom_call_target="tpu_custom_call" | custom-call | tf_op jit(solution)/shard_map/pallas_call | solution.py:55
  3.0 18.2 %all-to-all-start = ((bf16[64,32,256]{2,1,0:T(8,128)(2,1)}), bf16[64,32,256]{2,1,0:T(8,128)(2,1)S(1)}, u32[]{:S(2)}, u32[]{:S(2)}) async-start(bf16[64,32,256]{2,1,0:T(8,128)(2,1)} %bitcast.38), calls=%async_computation | async-start | bytes 2097152 | tf_op jit(solution)/shard_map/all_to_all | solution.py:114
  21.2 0.0 copy-done.4
  21.2 34.8 %all-gather = bf16[1024,256]{1,0:T(8,128)(2,1)} all-gather(bf16[64,256]{1,0:T(8,128)(2,1)S(1)} %bitcast.48), channel_id=2, replica_groups=mesh['x'=4,'z'=16,'col'=16] {'z'}, dimensions={0}, use_global_device_ids=true | all-gather | bytes 557056 | tf_op jit(solution)/shard_map/all_gather | solution.py:118
  56.0 0.0 copy-start
  56.0 0.0 all-to-all-done
  56.0 0.0 copy-start.2
  56.1 0.3 copy.9
  56.3 0.1 copy.12
  56.4 0.8 copy-done.2
  57.2 0.4 convolution_convert_fusion.1
  57.6 0.2 copy-done
  57.8 4.0 %shard_map.69 = bf16[16,64,256]{2,1,0:T(8,128)(2,1)S(1)} custom-call(bf16[4,16,32,256]{3,2,1,0:T(8,128)(2,1)S(1)} %bitcast.37, bf16[4096,256]{1,0:T(8,128)(2,1)S(1)} %copy-done), custom_call_target="tpu_custom_call" | custom-call | tf_op jit(solution)/shard_map/pallas_call | solution.py:92
  61.8 0.0 copy-start.1
  61.8 0.8 copy-done.1
  62.6 5.4 %all-to-all-start.1 = ((bf16[16,64,256]{2,1,0:T(8,128)(2,1)}), bf16[16,64,256]{2,1,0:T(8,128)(2,1)S(1)}, u32[]{:S(2)}, u32[]{:S(2)}) async-start(bf16[16,64,256]{2,1,0:T(8,128)(2,1)} %copy-done.1), calls=%async_computation.1 | async-start | bytes 1048576 | tf_op jit(solution)/shard_map/all_to_all | solution.py:124
  68.0 10.7 %all_gather.14 = bf16[1024,256]{1,0:T(8,128)(2,1)S(1)} all-gather(bf16[256,256]{1,0:T(8,128)(2,1)S(1)} %bitcast.44), channel_id=1, replica_groups=mesh['x'=4,'z'=16,'col'=16] {'x'}, dimensions={0}, use_global_device_ids=true | all-gather | bytes 655360 | tf_op jit(solution)/shard_map/all_gather | solution.py:127
  78.7 0.0 copy-start.3
  78.7 25.8 %all-gather.1 = bf16[1,1,1024,256]{3,2,1,0:T(8,128)(2,1)S(1)} all-gather(bf16[1,1,64,256]{3,2,1,0:T(8,128)(2,1)S(1)} %fusion.1), channel_id=3, replica_groups=mesh['x'=4,'z'=16,'col'=16] {'col'}, dimensions={2}, use_global_device_ids=true | all-gather | bytes 557056 | tf_op jit(solution)/shard_map/all_gather | solution.py:131
  104.5 0.0 all-to-all-done.1
  104.6 0.3 convolution_convert_fusion
  104.9 8.1 %all_to_all.15 = bf16[4,64,256]{2,1,0:T(8,128)(2,1)S(1)} all-to-all(bf16[4,64,256]{2,1,0:T(8,128)(2,1)S(1)} %bitcast.47), channel_id=1, replica_groups=mesh['x'=4,'z'=16,'col'=16] {'x'}, dimensions={0} | all-to-all | bytes 262144 | tf_op jit(solution)/shard_map/all_to_all | solution.py:19
  113.1 0.0 copy-done.3
  113.1 0.7 fusion.3
  (5 shorter events, 0.1 us)
Async XLA Ops:
  0.6 20.6 %copy-start.4 = (bf16[256,64]{0,1:T(8,128)(2,1)S(1)}, bf16[256,64]{0,1:T(8,128)(2,1)}, u32[]{:S(2)}) copy-start(bf16[256,64]{0,1:T(8,128)(2,1)} %param.5) | copy-start | bytes 98308
  3.0 53.0 %all-to-all-start = ((bf16[64,32,256]{2,1,0:T(8,128)(2,1)}), bf16[64,32,256]{2,1,0:T(8,128)(2,1)S(1)}, u32[]{:S(2)}, u32[]{:S(2)}) async-start(bf16[64,32,256]{2,1,0:T(8,128)(2,1)} %bitcast.38), calls=%async_computation | async-start | bytes 2097152 | tf_op jit(solution)/shard_map/all_to_all | solution.py:114
  56.0 1.7 %copy-start = (bf16[4096,256]{1,0:T(8,128)(2,1)S(1)}, bf16[4096,256]{1,0:T(8,128)(2,1)}, u32[]{:S(2)}) copy-start(bf16[4096,256]{1,0:T(8,128)(2,1)} %right_ref.1) | copy-start | bytes 6291460
  56.0 1.2 %copy-start.2 = (bf16[1024,256]{1,0:T(8,128)(2,1)S(1)}, bf16[1024,256]{1,0:T(8,128)(2,1)}, u32[]{:S(2)}) copy-start(bf16[1024,256]{1,0:T(8,128)(2,1)} %all-gather) | copy-start | bytes 1572868
  61.8 0.8 copy-start.1
  62.6 42.0 %all-to-all-start.1 = ((bf16[16,64,256]{2,1,0:T(8,128)(2,1)}), bf16[16,64,256]{2,1,0:T(8,128)(2,1)S(1)}, u32[]{:S(2)}, u32[]{:S(2)}) async-start(bf16[16,64,256]{2,1,0:T(8,128)(2,1)} %copy-done.1), calls=%async_computation.1 | async-start | bytes 1048576 | tf_op jit(solution)/shard_map/all_to_all | solution.py:124
  78.7 34.4 %copy-start.3 = (f32[64,256]{1,0:T(8,128)S(1)}, f32[64,256]{1,0:T(8,128)}, u32[]{:S(2)}) copy-start(f32[64,256]{1,0:T(8,128)} %param.9) | copy-start | bytes 196612
